TPU v7x, 256 devices: a whole 4x4x8 slice. The times are simulated.
256 devices in a mesh: role: 2 (over core), slot: 32 (over z, x), tp: 4 (over y).
Axes of the slice: x: 4, y: 4, z: 8, core: 2. Of those that a mesh axis runs over, the one named last changes fastest.
Arguments:
- queries: bfloat16 [2, 8192, 8192], P('role', 'slot', 'tp'), may hold values from -16 to 16
- cache_keys: bfloat16 [2, 256, 8, 256, 128], P('role', 'slot', 'tp'), may hold values from -16 to 16
- cache_values: bfloat16 [2, 256, 8, 256, 128], P('role', 'slot', 'tp'), may hold values from -6 to 6
- new_keys: bfloat16 [2, 8192, 1024], P('role', 'slot', 'tp'), may hold values from -16 to 16
- new_values: bfloat16 [2, 8192, 1024], P('role', 'slot', 'tp'), may hold values from -6 to 6
- out_weight: bfloat16 [2, 8192, 8192], P('role', 'tp'), may hold values from -0.0625 to 0.0625
- fork_src: int32 [256], P(('role', 'slot')), may hold values from 0 to 255, as said below
- cache_blocks: int32 [256], P('slot'), may hold values from 1 to 2, 320 in all
Outputs:
- layer_out: bfloat16 [2, 8192, 8192], P('role', ('slot', 'tp'))
Inputs may be any that keep to these rules, and one draw needn't show every extreme that they name: For every index a < 32, exactly 2 of the slots j with j // 8 = a have fork_src[j] = j (survivors); every other entry names a survivor. For all a and b, at most 1 slots j with j // 8 = a and fork_src[j] != j have fork_src[j] // 8 = b, and for every a some b has exactly 1.
All inputs are finite; a program needn't handle non-finite values. No bound on the sum of `cache_blocks` on one device may be relied on, other than what follows from the above.
Results may differ from a plain program's by a relative error of at most 0.0095.
Values may be sent and summed in bfloat16 or wider, within the bound.
No kernel may reach another device: no remote copies, remote signals or barrier semaphores. Data moves between devices by JAX's collectives and lax.ppermute only.
A program may use at most 128 MiB of HBM per device.

v0:
```python
import functools
import math

import jax
import jax.numpy as jnp
from jax import lax
from jax.experimental import pallas as pl
from jax.experimental.pallas import tpu as pltpu
from jax.sharding import PartitionSpec as P


BLK = 128
NX = 4
NZ = 8
NTP = 4
NODE = 8
STEP = 32
FAST = 2
META = 16

T_FROM = 0
T_RANK = 8
T_LEN = 16
T_FIT = 24
T_SIZE = 32

SMEM = pl.BlockSpec(memory_space=pltpu.SMEM)
VMEM = pl.BlockSpec(memory_space=pltpu.VMEM)
ANY = pl.BlockSpec(memory_space=pl.ANY)


def params(mib):
    return pltpu.CompilerParams(vmem_limit_bytes=mib << 20)


def zperm(d):
    return [(s, (s + NX * d) % (NX * NZ)) for s in range(NX * NZ)]


def xperm(d):
    return [(s, (s // NX) * NX + (s % NX + d) % NX) for s in range(NX * NZ)]


def yperm(d):
    return [(t, (t + d) % NTP) for t in range(NTP)]


def halves_perm(other, n_slot):
    pairs = []
    for role in range(2):
        for k in range(n_slot // 2):
            for h in range(2):
                dest = (h ^ other) * n_slot + role * (n_slot // 2) + k
                pairs.append((role * n_slot + 2 * k + h, dest))
    return pairs


def lane_row(values):
    lane = lax.broadcasted_iota(jnp.int32, (META, 128), 1)
    tile = jnp.zeros((META, 128), jnp.float32)
    for i, value in enumerate(values):
        tile = jnp.where(lane == i, value.astype(jnp.float32), tile)
    return tile.astype(jnp.bfloat16)


def column_counts(here, list_ref, col):
    base = here * NODE
    counts = [jnp.int32(0)] * NX
    for j in range(NODE):
        parent = list_ref[j]
        dist = (col - (parent // NODE) % NX + NX) % NX
        dist = jnp.where(parent == base + j, NX, dist)
        counts = [c + (dist == d).astype(jnp.int32) for d, c in enumerate(counts)]
    return counts


def pack_body(
    where_ref, mine_ref, other_ref, blocks_ref, keys_ref, values_ref,
    first_ref, second_ref, list_ref, sems,
):
    role = where_ref[0]
    here = where_ref[1]
    base = here * NODE
    count = jnp.int32(0)
    low = jnp.int32(0)
    high = jnp.int32(0)
    for j in range(NODE):
        h, k = divmod(j, NODE // 2)
        parent = jnp.where(role == h, mine_ref[k], other_ref[k])
        list_ref[j] = parent
        keep = parent == base + j
        low = jnp.where(keep & (count == 0), j, low)
        high = jnp.where(keep, j, high)
        count = count + keep.astype(jnp.int32)
    heads = keys_ref.shape[1]
    copies = []
    for b, out in enumerate((first_ref, second_ref)):
        for s, node in enumerate((low, high)):
            for kv, src in enumerate((keys_ref, values_ref)):
                for h in range(heads):
                    row = ((kv * 2 + s) * heads + h) * BLK
                    copies.append(
                        pltpu.make_async_copy(
                            src.at[node, h, pl.ds(b * BLK, BLK), :],
                            out.at[pl.ds(row, BLK), :],
                            sems.at[len(copies)],
                        )
                    )
    for c in copies:
        c.start()
    counts = column_counts(here, list_ref, here % NX)
    most = jnp.maximum(jnp.maximum(counts[0], counts[1]), jnp.maximum(counts[2], counts[3]))
    fit = (most <= FAST).astype(jnp.int32)
    rows = second_ref.shape[0]
    first_ref[rows : rows + META, :] = lane_row(
        (low, high, blocks_ref[low], blocks_ref[high], fit)
    )
    for c in copies:
        c.wait()


def pack(where, mine, other, blocks, keys, values):
    heads, _, dim = keys.shape[1:]
    rows = 4 * heads * BLK
    return pl.pallas_call(
        pack_body,
        out_shape=(
            pltpu.VMEM((rows + META, dim), keys.dtype),
            pltpu.VMEM((rows, dim), keys.dtype),
            jax.ShapeDtypeStruct((NODE,), jnp.int32),
        ),
        in_specs=[SMEM, SMEM, SMEM, SMEM, ANY, ANY],
        out_specs=(VMEM, VMEM, SMEM),
        scratch_shapes=[pltpu.SemaphoreType.DMA((8 * heads,))],
        compiler_params=params(2),
        name="pack",
    )(where, mine, other, blocks, keys, values)


def ring_step(pair):
    up, down = pair
    return lax.ppermute(up, "slot", zperm(1)), lax.ppermute(down, "slot", zperm(-1))


def ring_last(pair, up):
    if up:
        return lax.ppermute(pair[0], "slot", zperm(1))
    return lax.ppermute(pair[1], "slot", zperm(-1))


def ring_list(own, one, two, three, last):
    return [own, one[0], two[0], three[0], last, three[1], two[1], one[1]]


def issue_units(pick_ref, srcs, outs, size, sems):
    for d in range(NX):

        def unit(i, carry, d=d):
            u = d * FAST + i
            rel = pick_ref[u]
            rank = pick_ref[NX * FAST + u]
            for r in range(NZ):

                @pl.when(rel == r)
                def _(r=r):
                    for kv in range(2):
                        at = pl.multiple_of((kv * 2 + rank) * size, META)
                        to = pl.multiple_of((kv * 2 + i) * size, META)
                        pltpu.make_async_copy(
                            srcs[r].at[pl.ds(at, size), :],
                            outs[d].at[pl.ds(to, size), :],
                            sems.at[u * 2 + kv],
                        ).start()

            return carry

        lax.fori_loop(0, FAST, unit, 0)


def wait_units(srcs, outs, size, sems):
    def unit(n, carry):
        pltpu.make_async_copy(
            srcs[0].at[pl.ds(0, size), :], outs[0].at[pl.ds(0, size), :], sems.at[n]
        ).wait()
        return carry

    lax.fori_loop(0, NX * FAST * 2, unit, 0)


def select_first_body(where_ref, *refs):
    lists = refs[:NX]
    srcs = refs[NX : NX + NZ]
    outs = refs[NX + NZ : 2 * NX + NZ]
    pick_ref, meta_ref, wide_ref, ids_ref, sems, msem, ssem = refs[2 * NX + NZ :]
    size = outs[0].shape[0] // 4 // META * META
    here = where_ref[1]
    row = here // NX
    col = here % NX
    reads = []
    for rel in range(NZ):
        tile = srcs[rel].at[pl.ds(4 * size, META), :]
        reads.append(pltpu.make_async_copy(tile, meta_ref.at[rel], msem.at[rel]))
    for c in reads:
        c.start()
    for c in reads:
        c.wait()
    wide_ref[...] = meta_ref[...].astype(jnp.float32).astype(jnp.int32)
    spill = pltpu.make_async_copy(wide_ref, ids_ref, ssem)
    spill.start()
    spill.wait()
    for u in range(2 * NX * FAST):
        pick_ref[u] = 0
    for d in range(NX):
        base = (row * NX + (col + d) % NX) * NODE

        def scan(j, count, d=d, base=base):
            parent = lists[d][j]
            source = parent // NODE
            hit = (parent != base + j) & (source % NX == col)
            rel = (row - source // NX + NZ) % NZ

            @pl.when(hit & (count < FAST))
            def _():
                pick_ref[d * FAST + count] = rel
                pick_ref[NX * FAST + d * FAST + count] = (
                    parent % NODE == ids_ref[rel, 0, 1]
                ).astype(jnp.int32)

            return count + hit.astype(jnp.int32)

        lax.fori_loop(0, NODE, scan, jnp.int32(0))

    issue_units(pick_ref, srcs, outs, size, sems)
    fit = ids_ref[0, 0, 4]
    for rel in range(1, NZ):
        fit = jnp.minimum(fit, ids_ref[rel, 0, 4])
    for d in range(NX):
        sizes = []
        for i in range(FAST):
            u = d * FAST + i
            sizes.append(ids_ref[pick_ref[u], 0, 2 + pick_ref[NX * FAST + u]])
        outs[d][4 * size : 4 * size + META, :] = lane_row((sizes[0], sizes[1], fit))
    wait_units(srcs, outs, size, sems)


def select_first(where, lists, srcs):
    own = srcs[0]
    out = pltpu.VMEM(own.shape, own.dtype)
    return pl.pallas_call(
        select_first_body,
        out_shape=(out,) * NX + (jax.ShapeDtypeStruct((2 * NX * FAST,), jnp.int32),),
        in_specs=[SMEM] * (1 + NX) + [ANY] * NZ,
        out_specs=(VMEM,) * NX + (SMEM,),
        scratch_shapes=[
            pltpu.VMEM((NZ, META, 128), own.dtype),
            pltpu.VMEM((NZ, META, 128), jnp.int32),
            pltpu.SMEM((NZ, META, 128), jnp.int32),
            pltpu.SemaphoreType.DMA((NX * FAST * 2,)),
            pltpu.SemaphoreType.DMA((NZ,)),
            pltpu.SemaphoreType.DMA,
        ],
        compiler_params=params(2),
        name="select_first",
    )(where, *lists, *srcs)


def select_second_body(pick_ref, *refs):
    srcs = refs[:NZ]
    outs = refs[NZ : NZ + NX]
    sems = refs[NZ + NX]
    size = outs[0].shape[0] // 4

    issue_units(pick_ref, srcs, outs, size, sems)
    wait_units(srcs, outs, size, sems)


def select_second(picks, srcs):
    own = srcs[0]
    out = pltpu.VMEM(own.shape, own.dtype)
    return pl.pallas_call(
        select_second_body,
        out_shape=(out,) * NX,
        in_specs=[SMEM] + [ANY] * NZ,
        out_specs=(VMEM,) * NX,
        scratch_shapes=[pltpu.SemaphoreType.DMA((NX * FAST * 2,))],
        compiler_params=params(2),
        name="select_second",
    )(picks, *srcs)


def attend_node(n, tokens, scale, tp, q_ref, nk_ref, nv_ref, kbuf, vbuf, att_ref):
    heads, _, dim = kbuf.shape[1:]
    group = q_ref.shape[1] // (heads * dim)
    per = NODE // NTP
    at = pl.multiple_of(n * STEP, STEP)
    to = ((n // per - tp + NTP) % NTP) * per + n % per
    to = pl.multiple_of(to * STEP, STEP)
    rows = STEP * group
    f32 = jnp.float32
    nt = (((1,), (1,)), ((), ()))
    nn = (((1,), (0,)), ((), ()))
    step_of = lax.broadcasted_iota(jnp.int32, (rows, BLK), 0) % STEP
    step_ok = lax.broadcasted_iota(jnp.int32, (rows, BLK), 1) <= step_of
    pad = jnp.zeros((BLK - STEP, dim), kbuf.dtype)
    rate = scale * math.log2(math.e)
    logits = []
    for h in range(heads):
        base = h * group * dim
        q = jnp.concatenate(
            [q_ref[pl.ds(at, STEP), base + g * dim : base + (g + 1) * dim] for g in range(group)],
            axis=0,
        )
        nk = nk_ref[pl.ds(at, STEP), h * dim : (h + 1) * dim]
        k = jnp.concatenate([kbuf[n, h, :tokens], nk, pad], axis=0)
        logits.append(lax.dot_general(q, k, nt, preferred_element_type=f32))
    weights = []
    totals = []
    for h in range(heads):
        tiles = [logits[h][:, i : i + BLK] for i in range(0, tokens, BLK)]
        tiles.append(jnp.where(step_ok, logits[h][:, tokens:], -jnp.inf))
        top = tiles[0]
        for tile in tiles[1:]:
            top = jnp.maximum(top, tile)
        top = jnp.max(top, axis=1, keepdims=True)
        tiles = [jnp.exp2((tile - top) * rate) for tile in tiles]
        total = tiles[0]
        for tile in tiles[1:]:
            total = total + tile
        totals.append(jnp.sum(total, axis=1, keepdims=True))
        weights.append(jnp.concatenate([tile.astype(kbuf.dtype) for tile in tiles], axis=1))
    for h in range(heads):
        base = h * group * dim
        nv = nv_ref[pl.ds(at, STEP), h * dim : (h + 1) * dim]
        v = jnp.concatenate([vbuf[n, h, :tokens], nv, pad], axis=0)
        o = lax.dot_general(weights[h], v, nn, preferred_element_type=f32)
        o = (o * (1.0 / totals[h])).astype(att_ref.dtype)
        for g in range(group):
            att_ref[pl.ds(to, STEP), base + g * dim : base + (g + 1) * dim] = o[
                g * STEP : (g + 1) * STEP
            ]


def moved_copy(src, kv, rank, h, heads, j, b, buf, sem):
    at = pl.multiple_of(((kv * 2 + rank) * heads + h) * BLK, BLK)
    return pltpu.make_async_copy(
        src.at[pl.ds(at, BLK), :], buf.at[j, h, pl.ds(b * BLK, BLK), :], sem
    )


def early_body(scale, where_ref, list_ref, blocks_ref, q_ref, nk_ref, nv_ref, *refs):
    caches = refs[0:2]
    moved = refs[2 : 2 + NX]
    w_ref, att_ref, w0_ref, table_ref = refs[2 + NX : 6 + NX]
    kbuf, vbuf, meta_ref, wide_ref, ids_ref, sems, wsem, msem, ssem = refs[6 + NX :]
    bufs = (kbuf, vbuf)
    heads = kbuf.shape[1]
    here = where_ref[1]
    tp = where_ref[2]
    col = here % NX
    half = w0_ref.shape[1]
    reads = []
    for d in range(NX):
        at = moved[d].shape[0] - META
        reads.append(
            pltpu.make_async_copy(moved[d].at[pl.ds(at, META), :], meta_ref.at[d], msem.at[d])
        )
    for c in reads:
        c.start()

    def place(j, counts):
        parent = list_ref[j]
        moving = parent != here * NODE + j
        dist = jnp.where(moving, (col - (parent // NODE) % NX + NX) % NX, NX)
        rank = jnp.int32(0)
        after = []
        for d in range(NX):
            hit = dist == d
            rank = jnp.where(hit, counts[d], rank)
            after.append(counts[d] + hit.astype(jnp.int32))
        rank = jnp.minimum(rank, FAST - 1)
        table_ref[T_FROM + j] = dist
        table_ref[T_RANK + j] = rank

        @pl.when(dist == NX)
        def _():
            for kv in range(2):
                pltpu.make_async_copy(caches[kv].at[j], bufs[kv].at[j], sems.at[j, kv]).start()

        for d in range(NX):

            @pl.when(dist == d)
            def _(d=d):
                for kv in range(2):
                    for h in range(heads):
                        moved_copy(
                            moved[d], kv, rank, h, heads, j, 0, bufs[kv], sems.at[j, kv * heads + h]
                        ).start()

        return tuple(after)

    lax.fori_loop(0, NODE, place, (jnp.int32(0),) * NX)
    load = pltpu.make_async_copy(w_ref.at[:, pl.ds(0, half)], w0_ref, wsem)
    load.start()
    for c in reads:
        c.wait()
    wide_ref[...] = meta_ref[...].astype(jnp.float32).astype(jnp.int32)
    spill = pltpu.make_async_copy(wide_ref, ids_ref, ssem)
    spill.start()
    spill.wait()
    fit = ids_ref[0, 0, FAST]
    for d in range(1, NX):
        fit = jnp.minimum(fit, ids_ref[d, 0, FAST])
    for i in range(T_FIT, T_SIZE):
        table_ref[i] = fit

    def measure(j, carry):
        dist = table_ref[T_FROM + j]
        from_peer = ids_ref[jnp.minimum(dist, NX - 1), 0, table_ref[T_RANK + j]]
        table_ref[T_LEN + j] = jnp.where(dist == NX, blocks_ref[j], from_peer)
        return carry

    lax.fori_loop(0, NODE, measure, 0)

    def node(n, carry):
        local = table_ref[T_FROM + n] == NX
        blocks = table_ref[T_LEN + n]
        run = functools.partial(
            attend_node, n, scale=scale, tp=tp, q_ref=q_ref, nk_ref=nk_ref, nv_ref=nv_ref,
            kbuf=kbuf, vbuf=vbuf, att_ref=att_ref,
        )

        @pl.when(local)
        def _():
            for kv in range(2):
                pltpu.make_async_copy(caches[kv].at[n], bufs[kv].at[n], sems.at[n, kv]).wait()

        @pl.when(jnp.logical_not(local))
        def _():
            for kv in range(2):
                for h in range(heads):
                    moved_copy(
                        moved[0], kv, 0, h, heads, n, 0, bufs[kv], sems.at[n, kv * heads + h]
                    ).wait()

        @pl.when(local & (blocks == 2))
        def _():
            run(tokens=2 * BLK)

        @pl.when(blocks == 1)
        def _():
            run(tokens=BLK)

        return carry

    lax.fori_loop(0, NODE, node, 0)
    load.wait()


def early(where, own_list, blocks, queries, new_keys, new_values, keys, values, moved, weight):
    dim = keys.shape[3]
    inner, cols = weight.shape
    half = pltpu.VMEM((inner, cols // 2), weight.dtype)
    return pl.pallas_call(
        functools.partial(early_body, float(dim) ** -0.5),
        out_shape=(
            pltpu.VMEM(queries.shape, queries.dtype),
            half,
            jax.ShapeDtypeStruct((T_SIZE,), jnp.int32),
        ),
        in_specs=[SMEM, SMEM, SMEM, VMEM, VMEM, VMEM] + [ANY] * (3 + NX),
        out_specs=(VMEM, VMEM, SMEM),
        scratch_shapes=[
            pltpu.VMEM(keys.shape, keys.dtype),
            pltpu.VMEM(keys.shape, keys.dtype),
            pltpu.VMEM((NX, META, 128), keys.dtype),
            pltpu.VMEM((NX, META, 128), jnp.int32),
            pltpu.SMEM((NX, META, 128), jnp.int32),
            pltpu.SemaphoreType.DMA((NODE, 2 * keys.shape[1])),
            pltpu.SemaphoreType.DMA,
            pltpu.SemaphoreType.DMA((NX,)),
            pltpu.SemaphoreType.DMA,
        ],
        compiler_params=params(8),
        name="early",
    )(where, own_list, blocks, queries, new_keys, new_values, keys, values, *moved, weight)


def project_half(chunk, tile, att_ref, w_ref, own_ref, relay_a, relay_b, da, db, ca, cb):
    part, half = relay_a.shape
    base = chunk * half

    def step(side, c, carry):
        at = pl.multiple_of(c * tile, tile)
        cols = pl.ds(pl.multiple_of(side * half + at, tile), tile)
        far = pl.ds(pl.multiple_of(base + at, tile), tile)
        res = jnp.dot(att_ref[...], w_ref[:, cols], preferred_element_type=jnp.float32)
        res = res.astype(own_ref.dtype)
        own_ref[:, cols] = res[:part]
        (ca, db)[side][:, far] = res[part : 2 * part]
        (relay_a, relay_b)[side][:, pl.ds(at, tile)] = res[2 * part : 3 * part]
        (da, cb)[side][:, far] = res[3 * part :]
        return carry

    for side in range(2):
        lax.fori_loop(0, half // tile, functools.partial(step, side), 0)


def late_body(scale, tile, where_ref, table_ref, q_ref, nk_ref, nv_ref, *refs):
    firsts = refs[:NX]
    seconds = refs[NX : 2 * NX]
    old_ref, w0_ref, w_ref, att_ref, w1_ref = refs[2 * NX : 2 * NX + 5]
    outs = refs[2 * NX + 5 : 2 * NX + 12]
    kbuf, vbuf, sems, wsem = refs[2 * NX + 12 :]
    del old_ref
    bufs = (kbuf, vbuf)
    heads = kbuf.shape[1]
    tp = where_ref[2]
    half = w1_ref.shape[1]

    def is_late(n):
        return (table_ref[T_FROM + n] < NX) & (table_ref[T_LEN + n] == 2)

    def copies(n, d, rank):
        for b, group in enumerate((firsts, seconds)):
            for kv in range(2):
                for h in range(heads):
                    yield moved_copy(
                        group[d], kv, rank, h, heads, n, b, bufs[kv],
                        sems.at[n, (b * 2 + kv) * heads + h],
                    )

    def start(n, carry):
        for d in range(NX):

            @pl.when(is_late(n) & (table_ref[T_FROM + n] == d))
            def _(d=d):
                for c in copies(n, d, table_ref[T_RANK + n]):
                    c.start()

        return carry

    lax.fori_loop(0, NODE, start, 0)
    load = pltpu.make_async_copy(w_ref.at[:, pl.ds(half, half)], w1_ref, wsem)
    load.start()

    def node(n, carry):
        @pl.when(is_late(n))
        def _():
            for c in copies(n, 0, 0):
                c.wait()
            attend_node(n, 2 * BLK, scale, tp, q_ref, nk_ref, nv_ref, kbuf, vbuf, att_ref)

        return carry

    lax.fori_loop(0, NODE, node, 0)
    project_half(0, tile, att_ref, w0_ref, *outs)
    load.wait()


def late(where, table, queries, new_keys, new_values, moved, att, weight0, weight, shape, tile):
    dtype = queries.dtype
    part = att.shape[0] // NTP
    inner, half = weight0.shape
    wide = pltpu.VMEM((part, half), dtype)
    slim = pltpu.VMEM((part, half // 2), dtype)
    return pl.pallas_call(
        functools.partial(late_body, float(shape[3]) ** -0.5, tile),
        out_shape=(pltpu.VMEM(att.shape, dtype), pltpu.VMEM((inner, half), dtype))
        + (wide, slim, slim, wide, wide, wide, wide),
        in_specs=[SMEM, SMEM, VMEM, VMEM, VMEM] + [ANY] * (2 * NX) + [VMEM, VMEM, ANY],
        out_specs=(VMEM,) * 9,
        scratch_shapes=[
            pltpu.VMEM(shape, dtype),
            pltpu.VMEM(shape, dtype),
            pltpu.SemaphoreType.DMA((NODE, 4 * shape[1])),
            pltpu.SemaphoreType.DMA,
        ],
        input_output_aliases={5 + 2 * NX: 0},
        compiler_params=params(8),
        name="late",
    )(where, table, queries, new_keys, new_values, *moved, att, weight0, weight)


def project_body(tile, att_ref, w_ref, da0, db0, ca0, cb0, own_ref, ra, rb, da, db, ca, cb):
    del da0, db0, ca0, cb0
    project_half(1, tile, att_ref, w_ref, own_ref, ra, rb, da, db, ca, cb)


def project(att, weight, shared, tile):
    part = att.shape[0] // NTP
    half = weight.shape[1]
    wide = pltpu.VMEM((part, half), att.dtype)
    slim = pltpu.VMEM((part, half // 2), att.dtype)
    return pl.pallas_call(
        functools.partial(project_body, tile),
        out_shape=(wide, slim, slim, wide, wide, wide, wide),
        in_specs=[VMEM] * 6,
        out_specs=(VMEM,) * 7,
        input_output_aliases={2 + i: 3 + i for i in range(4)},
        compiler_params=params(6),
        name="project",
    )(att, weight, *shared)


def combine_body(base_ref, low_ref, high_ref, out_ref):
    half = low_ref.shape[1]
    for i, ref in enumerate((low_ref, high_ref)):
        cols = slice(i * half, (i + 1) * half)
        total = base_ref[:, cols].astype(jnp.float32) + ref[...].astype(jnp.float32)
        out_ref[:, cols] = total.astype(out_ref.dtype)


def combine(base, low, high):
    return pl.pallas_call(
        combine_body,
        out_shape=pltpu.VMEM(base.shape, base.dtype),
        in_specs=[VMEM] * 3,
        out_specs=VMEM,
        compiler_params=params(2),
        name="combine",
    )(base, low, high)


def finish_body(own0, own1, da, db, fa, fb, out_ref):
    half = own0.shape[1] // 2
    for c, own in enumerate((own0, own1)):
        here = slice(c * half, (c + 1) * half)
        for side, (near, far) in enumerate(((da, fa), (db, fb))):
            cols = slice(side * half, (side + 1) * half)
            total = own[:, cols].astype(jnp.float32) + near[:, here].astype(jnp.float32)
            total = total + far[:, here].astype(jnp.float32)
            at = 2 * c * half + side * half
            out_ref[:, at : at + half] = total.astype(out_ref.dtype)


def finish(*args):
    part, half = args[0].shape
    return pl.pallas_call(
        finish_body,
        out_shape=jax.ShapeDtypeStruct((part, 2 * half), args[0].dtype),
        in_specs=[VMEM] * 6,
        out_specs=VMEM,
        compiler_params=params(4),
        name="finish",
    )(*args)


def general(
    where, mine, other, queries, keys, values, new_keys, new_values, weight, cache_blocks
):
    n_slot = lax.axis_size("slot")
    slot_here = lax.axis_index("slot")
    tp_here = lax.axis_index("tp")
    heads, tokens, dim = keys.shape[1:]
    rows, width = queries.shape
    group = width // (heads * dim)
    scale = float(dim) ** -0.5
    f32 = jnp.float32
    first, second, own = pack(where, mine, other, cache_blocks, keys, values)
    size = second.shape[0]
    each = heads * BLK

    def turn(t, carry):
        buf, got, blocks = carry
        from_slot = (slot_here - t + n_slot) % n_slot
        ids = buf[size].astype(jnp.int32)

        def take(j, state):
            got, blocks = state
            hit = (own[j] != slot_here * NODE + j) & (own[j] // NODE == from_slot)
            rank = (own[j] % NODE == ids[1]).astype(jnp.int32)

            def put(state):
                got, blocks = state
                for b in range(2):
                    for kv in range(2):
                        start = b * (size + META) + (kv * 2 + rank) * each
                        unit = lax.dynamic_slice_in_dim(buf, start, each)
                        got = lax.dynamic_update_slice(got, unit[None, None, None], (j, kv, b, 0, 0))
                return got, lax.dynamic_update_slice(blocks, ids[2 + rank][None], (j,))

            return lax.cond(hit, put, lambda state: state, (got, blocks))

        got, blocks = lax.fori_loop(0, NODE, take, (got, blocks))
        pairs = [(s, (s + 1) % n_slot) for s in range(n_slot)]
        return lax.ppermute(buf, "slot", pairs), got, blocks

    local = jnp.stack([keys, values], axis=1).reshape(NODE, 2, heads, 2, BLK, dim)
    local = local.transpose(0, 1, 3, 2, 4, 5).reshape(NODE, 2, 2, each, dim)
    carry = (jnp.concatenate([first, second]), local, cache_blocks)
    got, blocks = lax.fori_loop(0, n_slot, turn, carry)[1:]
    row_at = lax.broadcasted_iota(jnp.int32, (STEP * group, 1), 0) // group
    step_ok = lax.broadcasted_iota(jnp.int32, (1, STEP), 1) <= row_at
    token_at = lax.broadcasted_iota(jnp.int32, (1, tokens), 1)

    def unit(n, att):
        j, h = n // heads, n % heads

        def cut(a, wide):
            return lax.dynamic_slice(a, (j * STEP, h * wide), (STEP, wide))

        def cache(kv):
            return lax.dynamic_slice(got, (j, kv, 0, h * BLK, 0), (1, 1, 2, BLK, dim)).reshape(
                tokens, dim
            )

        q = cut(queries, group * dim).reshape(STEP * group, dim)
        k = jnp.concatenate([cache(0), cut(new_keys, dim)])
        v = jnp.concatenate([cache(1), cut(new_values, dim)])
        ok = jnp.concatenate(
            [jnp.broadcast_to(token_at < blocks[j] * BLK, (STEP * group, tokens)), step_ok], axis=1
        )
        logits = jnp.dot(q, k.T, preferred_element_type=f32) * scale
        logits = jnp.where(ok, logits, -jnp.inf)
        weights = jnp.exp(logits - jnp.max(logits, axis=1, keepdims=True))
        out = jnp.dot(weights.astype(v.dtype), v, preferred_element_type=f32)
        out = out / jnp.sum(weights, axis=1, keepdims=True)
        out = out.astype(att.dtype).reshape(STEP, group * dim)
        return lax.dynamic_update_slice(att, out, (j * STEP, h * group * dim))

    att = lax.fori_loop(0, NODE * heads, unit, jnp.zeros_like(queries))
    part = rows // NTP
    cols = weight.shape[1]
    tile = 512

    def piece(i):
        mine = lax.dynamic_slice_in_dim(att, (tp_here + i) % NTP * part, part)

        def column(c, total):
            w = lax.dynamic_slice_in_dim(weight, c * tile, tile, axis=1)
            res = jnp.dot(mine, w, preferred_element_type=f32)
            return lax.dynamic_update_slice(total, res, (0, c * tile))

        return lax.fori_loop(0, cols // tile, column, jnp.zeros((part, cols), f32))

    def pass_on(k, total):
        return lax.ppermute(total, "tp", yperm(1)) + piece(2 * NTP - 1 - k)

    total = lax.fori_loop(0, NTP, pass_on, jnp.zeros((part, cols), f32))
    return total.astype(att.dtype)


def shards(
    queries, cache_keys, cache_values, new_keys, new_values, out_weight, fork_src, cache_blocks
):
    queries, keys, values = queries[0], cache_keys[0], cache_values[0]
    new_keys, new_values, weight = new_keys[0], new_values[0], out_weight[0]
    n_slot = lax.axis_size("slot")
    where = jnp.stack([lax.axis_index(name).astype(jnp.int32) for name in ("role", "slot", "tp")])

    mine = lax.ppermute(fork_src, ("role", "slot"), halves_perm(0, n_slot))
    other = lax.ppermute(fork_src, ("role", "slot"), halves_perm(1, n_slot))
    first, second, own_list = pack(where, mine, other, cache_blocks, keys, values)
    first1 = ring_step((first, first))
    second1 = ring_step((second, second))
    lists = [own_list]
    for d in (1, 2, 3):
        lists.append(lax.ppermute(own_list, "slot", xperm(-d)))
    first2 = ring_step(first1)
    second2 = ring_step(second1)
    first3 = ring_step(first2)
    second3 = ring_step(second2)
    got_first = ring_list(first, first1, first2, first3, ring_last(first3, True))
    got_second = ring_list(second, second1, second2, second3, ring_last(second3, False))
    *outs_first, picks = select_first(where, lists, got_first)
    moved = [outs_first[0]]
    for d in (1, 2, 3):
        moved.append(lax.ppermute(outs_first[d], "slot", xperm(d)))
    outs_second = select_second(picks, got_second)
    att, weight0, table = early(
        where, own_list, cache_blocks, queries, new_keys, new_values, keys, values, moved,
        weight,
    )
    moved = moved + [outs_second[0]]
    for d in (1, 2, 3):
        moved.append(lax.ppermute(outs_second[d], "slot", xperm(d)))
    att, weight1, own0, relay_a0, relay_b0, *shared = late(
        where, table, queries, new_keys, new_values, moved, att, weight0, weight, keys.shape, 512
    )
    up, down = yperm(1), yperm(-1)
    relay_a0 = lax.ppermute(relay_a0, "tp", up)
    relay_b0 = lax.ppermute(relay_b0, "tp", down)
    own1, relay_a1, relay_b1, da, db, ca, cb = project(att, weight1, shared, 512)
    relay_a1 = lax.ppermute(relay_a1, "tp", up)
    relay_b1 = lax.ppermute(relay_b1, "tp", down)
    da = lax.ppermute(da, "tp", down)
    db = lax.ppermute(db, "tp", up)
    far_a = lax.ppermute(combine(ca, relay_a0, relay_a1), "tp", up)
    far_b = lax.ppermute(combine(cb, relay_b0, relay_b1), "tp", down)
    out = finish(own0, own1, da, db, far_a, far_b)
    args = (where, mine, other, queries, keys, values, new_keys, new_values, weight, cache_blocks)
    out = lax.cond(table[T_FIT] == 1, lambda o, *_: o, lambda o, *a: general(*a), out, *args)
    return out[None]


def solution(mesh):
    in_specs = (
        P("role", "slot", "tp"),
        P("role", "slot", "tp", None, None),
        P("role", "slot", "tp", None, None),
        P("role", "slot", "tp"),
        P("role", "slot", "tp"),
        P("role", "tp", None),
        P(("role", "slot")),
        P("slot"),
    )
    out_specs = P("role", ("slot", "tp"), None)

    return jax.shard_map(shards, mesh=mesh, in_specs=in_specs, out_specs=out_specs, check_vma=False)
```

profile of v0, /device:TPU:102, one launch (start us, length us, event | category | flops | bytes accessed | tf_op | source)
XLA Modules:
  0.0 149.0 jit_solution(10026261630460782623)
XLA Ops:
  0.7 1.9 %collective-permute-start.2 = (s32[4]{0:T(128)}, s32[4]{0:T(128)S(1)}, u32[]{:S(2)}, u32[]{:S(2)}) collective-permute-start(s32[4]{0:T(128)} %param.28), channel_id=1, source_target_pairs={{0,0},{4,128},{8,4},{12,132},{16,8},{20,136},{24,12},{28,140},{32,... | collective-permute-start | bytes 56 | tf_op jit(solution)/shard_map/ppermute | solution.py:751
  2.8 8.3 %collective-permute-done.2.mine_ref = s32[4]{0:T(128)S(1)} collective-permute-done((s32[4]{0:T(128)}, s32[4]{0:T(128)S(1)}, u32[]{:S(2)}, u32[]{:S(2)}) %collective-permute-start.2) | collective-permute-done | bytes 48 | tf_op jit(solution)/shard_map/ppermute | solution.py:751
  11.1 2.4 %pack.3 = (bf16[1040,128]{1,0:T(8,128)(2,1)S(1)}, bf16[1024,128]{1,0:T(8,128)(2,1)S(1)}, s32[8]{0:T(128)S(1)}) custom-call(s32[3]{0:T(128)S(1)} %pad_add_fusion.where_ref, s32[4]{0:T(128)S(1)} %collective-permute-done.2.mine_ref, s32[4]{0:T(128)S(1)} %collective-permute-done.3.other_ref, s32[8]{0:T(128)S(1)} %copy.81.blocks_ref, ...), custom_call_target="tpu_custom_call" | custom-call | tf_op jit(solution)/shard_map/pack/pallas_call | solution.py:125
  13.4 1.7 %collective-permute-start.7 = (bf16[1040,128]{1,0:T(8,128)(2,1)S(1)}, bf16[1040,128]{1,0:T(8,128)(2,1)S(1)}, u32[]{:S(2)}, u32[]{:S(2)}) collective-permute-start(bf16[1040,128]{1,0:T(8,128)(2,1)S(1)} %get-tuple-element.1043.refs_4_), channel_id=1, source_target_pairs={{0,16},{4,20},{8,24},{12,28},{16,32},{20,36},{24,40},{28,44},{32,4... | collective-permute-start | bytes 798728 | tf_op jit(solution)/shard_map/ppermute | solution.py:142
  15.5 6.0 %collective-permute-done.7.refs_5_ = bf16[1040,128]{1,0:T(8,128)(2,1)S(1)} collective-permute-done((bf16[1040,128]{1,0:T(8,128)(2,1)S(1)}, bf16[1040,128]{1,0:T(8,128)(2,1)S(1)}, u32[]{:S(2)}, u32[]{:S(2)}) %collective-permute-start.7) | collective-permute-done | bytes 266272 | tf_op jit(solution)/shard_map/ppermute | solution.py:142
  21.5 3.7 %collective-permute-start.8 = (bf16[1040,128]{1,0:T(8,128)(2,1)S(1)}, bf16[1040,128]{1,0:T(8,128)(2,1)S(1)}, u32[]{:S(2)}, u32[]{:S(2)}) collective-permute-start(bf16[1040,128]{1,0:T(8,128)(2,1)S(1)} %collective-permute-done.7.refs_5_), channel_id=1, source_target_pairs={{0,16},{4,20},{8,24},{12,28},{16,32},{20,36},{24,40},{28,44},{32,4... | collective-permute-start | bytes 798728 | tf_op jit(solution)/shard_map/ppermute | solution.py:142
  25.5 5.8 %collective-permute-done.8.refs_6_ = bf16[1040,128]{1,0:T(8,128)(2,1)S(1)} collective-permute-done((bf16[1040,128]{1,0:T(8,128)(2,1)S(1)}, bf16[1040,128]{1,0:T(8,128)(2,1)S(1)}, u32[]{:S(2)}, u32[]{:S(2)}) %collective-permute-start.8) | collective-permute-done | bytes 266272 | tf_op jit(solution)/shard_map/ppermute | solution.py:142
  31.3 3.7 %collective-permute-start.9 = (bf16[1040,128]{1,0:T(8,128)(2,1)S(1)}, bf16[1040,128]{1,0:T(8,128)(2,1)S(1)}, u32[]{:S(2)}, u32[]{:S(2)}) collective-permute-start(bf16[1040,128]{1,0:T(8,128)(2,1)S(1)} %collective-permute-done.8.refs_6_), channel_id=1, source_target_pairs={{0,16},{4,20},{8,24},{12,28},{16,32},{20,36},{24,40},{28,44},{32,4... | collective-permute-start | bytes 798728 | tf_op jit(solution)/shard_map/ppermute | solution.py:142
  37.0 4.3 %collective-permute-done.12.refs_10_ = bf16[1040,128]{1,0:T(8,128)(2,1)S(1)} collective-permute-done((bf16[1040,128]{1,0:T(8,128)(2,1)S(1)}, bf16[1040,128]{1,0:T(8,128)(2,1)S(1)}, u32[]{:S(2)}, u32[]{:S(2)}) %collective-permute-start.12) | collective-permute-done | bytes 266272 | tf_op jit(solution)/shard_map/ppermute | solution.py:142
  41.8 3.7 %collective-permute-start.10 = (bf16[1040,128]{1,0:T(8,128)(2,1)S(1)}, bf16[1040,128]{1,0:T(8,128)(2,1)S(1)}, u32[]{:S(2)}, u32[]{:S(2)}) collective-permute-start(bf16[1040,128]{1,0:T(8,128)(2,1)S(1)} %collective-permute-done.9.refs_7_), channel_id=1, source_target_pairs={{0,16},{4,20},{8,24},{12,28},{16,32},{20,36},{24,40},{28,44},{32,4... | collective-permute-start | bytes 798728 | tf_op jit(solution)/shard_map/ppermute | solution.py:147
  45.5 1.9 %collective-permute-done.17.refs_1_ = bf16[1024,128]{1,0:T(8,128)(2,1)S(1)} collective-permute-done((bf16[1024,128]{1,0:T(8,128)(2,1)S(1)}, bf16[1024,128]{1,0:T(8,128)(2,1)S(1)}, u32[]{:S(2)}, u32[]{:S(2)}) %collective-permute-start.17) | collective-permute-done | bytes 262176 | tf_op jit(solution)/shard_map/ppermute | solution.py:142
  47.4 3.7 %collective-permute-start.18 = (bf16[1024,128]{1,0:T(8,128)(2,1)S(1)}, bf16[1024,128]{1,0:T(8,128)(2,1)S(1)}, u32[]{:S(2)}, u32[]{:S(2)}) collective-permute-start(bf16[1024,128]{1,0:T(8,128)(2,1)S(1)} %collective-permute-done.17.refs_1_), channel_id=1, source_target_pairs={{0,16},{4,20},{8,24},{12,28},{16,32},{20,36},{24,40},{28,44},{32,4... | collective-permute-start | bytes 786440 | tf_op jit(solution)/shard_map/ppermute | solution.py:142
  52.8 3.2 %collective-permute-done.4.refs_1_ = s32[8]{0:T(128)S(1)} collective-permute-done((s32[8]{0:T(128)S(1)}, s32[8]{0:T(128)S(1)}, u32[]{:S(2)}, u32[]{:S(2)}) %collective-permute-start.4) | collective-permute-done | bytes 64 | tf_op jit(solution)/shard_map/ppermute | solution.py:758
  56.4 4.7 %collective-permute-done.5.refs_2_ = s32[8]{0:T(128)S(1)} collective-permute-done((s32[8]{0:T(128)S(1)}, s32[8]{0:T(128)S(1)}, u32[]{:S(2)}, u32[]{:S(2)}) %collective-permute-start.5) | collective-permute-done | bytes 64 | tf_op jit(solution)/shard_map/ppermute | solution.py:758
  61.3 3.3 %collective-permute-done.6.refs_3_ = s32[8]{0:T(128)S(1)} collective-permute-done((s32[8]{0:T(128)S(1)}, s32[8]{0:T(128)S(1)}, u32[]{:S(2)}, u32[]{:S(2)}) %collective-permute-start.6) | collective-permute-done | bytes 64 | tf_op jit(solution)/shard_map/ppermute | solution.py:758
  64.6 6.0 %select_first.1 = (bf16[1040,128]{1,0:T(8,128)(2,1)S(1)}, bf16[1040,128]{1,0:T(8,128)(2,1)S(1)}, bf16[1040,128]{1,0:T(8,128)(2,1)S(1)}, bf16[1040,128]{1,0:T(8,128)(2,1)S(1)}, s32[16]{0:T(128)S(1)}) custom-call(s32[3]{0:T(128)S(1)} %pad_add_fusion.where_ref, s32[8]{0:T(128)S(1)} %get-tuple-element.1042.refs_0_.list_ref, ...), custom_call_target="tpu_custom_call" | custom-call | tf_op jit(solution)/shard_map/select_first/pallas_call | solution.py:249
  72.2 3.2 %collective-permute-start.19 = (bf16[1024,128]{1,0:T(8,128)(2,1)S(1)}, bf16[1024,128]{1,0:T(8,128)(2,1)S(1)}, u32[]{:S(2)}, u32[]{:S(2)}) collective-permute-start(bf16[1024,128]{1,0:T(8,128)(2,1)S(1)} %collective-permute-done.18.refs_2_), channel_id=1, source_target_pairs={{0,16},{4,20},{8,24},{12,28},{16,32},{20,36},{24,40},{28,44},{32,4... | collective-permute-start | bytes 786440 | tf_op jit(solution)/shard_map/ppermute | solution.py:142
  76.4 2.9 %collective-permute-done.19.refs_3_ = bf16[1024,128]{1,0:T(8,128)(2,1)S(1)} collective-permute-done((bf16[1024,128]{1,0:T(8,128)(2,1)S(1)}, bf16[1024,128]{1,0:T(8,128)(2,1)S(1)}, u32[]{:S(2)}, u32[]{:S(2)}) %collective-permute-start.19) | collective-permute-done | bytes 262176 | tf_op jit(solution)/shard_map/ppermute | solution.py:142
  79.3 3.7 %collective-permute-done.23.refs_4_ = bf16[1024,128]{1,0:T(8,128)(2,1)S(1)} collective-permute-done((bf16[1024,128]{1,0:T(8,128)(2,1)S(1)}, bf16[1024,128]{1,0:T(8,128)(2,1)S(1)}, u32[]{:S(2)}, u32[]{:S(2)}) %collective-permute-start.23) | collective-permute-done | bytes 262176 | tf_op jit(solution)/shard_map/ppermute | solution.py:148
  83.0 2.6 %select_second.1 = (bf16[1024,128]{1,0:T(8,128)(2,1)S(1)}, bf16[1024,128]{1,0:T(8,128)(2,1)S(1)}, bf16[1024,128]{1,0:T(8,128)(2,1)S(1)}, bf16[1024,128]{1,0:T(8,128)(2,1)S(1)}) custom-call(s32[16]{0:T(128)S(1)} %get-tuple-element.1049.pick_ref, bf16[1024,128]{1,0:T(8,128)(2,1)S(1)} %get-tuple-element.1050.refs_0_, ...), custom_call_target="tpu_custom_call" | custom-call | tf_op jit(solution)/shard_map/select_second/pallas_call | solution.py:280
  85.7 2.5 %collective-permute-start.25 = (bf16[1024,128]{1,0:T(8,128)(2,1)S(1)}, bf16[1024,128]{1,0:T(8,128)(2,1)S(1)}, u32[]{:S(2)}, u32[]{:S(2)}) collective-permute-start(bf16[1024,128]{1,0:T(8,128)(2,1)S(1)} %get-tuple-element.1053), channel_id=1, source_target_pairs={{0,8},{4,12},{8,0},{12,4},{16,24},{20,28},{24,16},{28,20},{32,40},... | collective-permute-start | bytes 786440 | tf_op jit(solution)/shard_map/ppermute | solution.py:776
  88.2 4.4 %collective-permute-done.16.refs_5_.refs_3_ = bf16[1040,128]{1,0:T(8,128)(2,1)S(1)} collective-permute-done((bf16[1040,128]{1,0:T(8,128)(2,1)S(1)}, bf16[1040,128]{1,0:T(8,128)(2,1)S(1)}, u32[]{:S(2)}, u32[]{:S(2)}) %collective-permute-start.16) | collective-permute-done | bytes 266272 | tf_op jit(solution)/shard_map/ppermute | solution.py:768
  92.7 9.5 %early.1 = (bf16[256,2048]{1,0:T(8,128)(2,1)S(1)}, bf16[2048,4096]{1,0:T(8,128)(2,1)S(1)}, s32[32]{0:T(128)S(1)}) custom-call(s32[3]{0:T(128)S(1)} %pad_add_fusion.where_ref, s32[8]{0:T(128)S(1)} %get-tuple-element.1042.refs_0_.list_ref, s32[8]{0:T(128)S(1)} %copy.81.blocks_ref, bf16[256,2048]{1,0:T(8,128)(2,1)S(1)} %bitcast.71, ...), custom_call_target="tpu_custom_call" | custom-call | tf_op jit(solution)/shard_map/early/pallas_call | solution.py:463
  102.2 8.3 %late.1 = (bf16[256,2048]{1,0:T(8,128)(2,1)S(1)}, bf16[2048,4096]{1,0:T(8,128)(2,1)S(1)}, bf16[64,4096]{1,0:T(8,128)(2,1)S(1)}, bf16[64,2048]{1,0:T(8,128)(2,1)S...) custom-call(s32[3]{0:T(128)S(1)} %pad_add_fusion.where_ref, ...), custom_call_target="tpu_custom_call", output_to_operand_aliasing={{0}: (13, {})} | custom-call | tf_op jit(solution)/shard_map/late/pallas_call | solution.py:566
  110.5 5.7 %project.1 = (bf16[64,4096]{1,0:T(8,128)(2,1)S(1)}, bf16[64,2048]{1,0:T(8,128)(2,1)S(1)}, bf16[64,2048]{1,0:T(8,128)(2,1)S(1)}, bf16[64,4096]{1,0:T(8,128)(2,1)S...) custom-call(bf16[256,2048]{1,0:T(8,128)(2,1)S(1)} %get-tuple-element, ...), custom_call_target="tpu_custom_call", output_to_operand_aliasing={{3}: (2, {}), {4}: (3, {}), {5}: (4, {}), {6}: (5, {})} | custom-call | tf_op jit(solution)/shard_map/project/pallas_call | solution.py:594
  116.2 3.1 %collective-permute-start.33 = (bf16[64,2048]{1,0:T(8,128)(2,1)S(1)}, bf16[64,2048]{1,0:T(8,128)(2,1)S(1)}, u32[]{:S(2)}, u32[]{:S(2)}) collective-permute-start(bf16[64,2048]{1,0:T(8,128)(2,1)S(1)} %get-tuple-element.1072), channel_id=1, source_target_pairs={{0,3},{1,0},{2,1},{3,2},{4,7},{5,4},{6,5},{7,6},{8,11},{9,8},{10,9... | collective-permute-start | bytes 786440 | tf_op jit(solution)/shard_map/ppermute | solution.py:785
  121.4 3.2 %collective-permute-start.27 = (bf16[64,4096]{1,0:T(8,128)(2,1)S(1)}, bf16[64,4096]{1,0:T(8,128)(2,1)S(1)}, u32[]{:S(2)}, u32[]{:S(2)}) collective-permute-start(bf16[64,4096]{1,0:T(8,128)(2,1)S(1)} %get-tuple-element.1065), channel_id=1, source_target_pairs={{0,3},{1,0},{2,1},{3,2},{4,7},{5,4},{6,5},{7,6},{8,11},{9,8},{10,9... | collective-permute-start | bytes 1572872 | tf_op jit(solution)/shard_map/ppermute | solution.py:786
  127.0 4.6 %collective-permute-done.32.low_ref = bf16[64,2048]{1,0:T(8,128)(2,1)S(1)} collective-permute-done((bf16[64,2048]{1,0:T(8,128)(2,1)S(1)}, bf16[64,2048]{1,0:T(8,128)(2,1)S(1)}, u32[]{:S(2)}, u32[]{:S(2)}) %collective-permute-start.32) | collective-permute-done | bytes 262176 | tf_op jit(solution)/shard_map/ppermute | solution.py:782
  131.7 3.8 %collective-permute-start.34 = (bf16[64,4096]{1,0:T(8,128)(2,1)S(1)}, bf16[64,4096]{1,0:T(8,128)(2,1)S(1)}, u32[]{:S(2)}, u32[]{:S(2)}) collective-permute-start(bf16[64,4096]{1,0:T(8,128)(2,1)S(1)} %combine.3), channel_id=1, source_target_pairs={{0,3},{1,0},{2,1},{3,2},{4,7},{5,4},{6,5},{7,6},{8,11},{9,8},{10,9... | collective-permute-start | bytes 1572872 | tf_op jit(solution)/shard_map/ppermute | solution.py:789
  138.2 3.9 %collective-permute-done.28.db = bf16[64,4096]{1,0:T(8,128)(2,1)S(1)} collective-permute-done((bf16[64,4096]{1,0:T(8,128)(2,1)S(1)}, bf16[64,4096]{1,0:T(8,128)(2,1)S(1)}, u32[]{:S(2)}, u32[]{:S(2)}) %collective-permute-start.28) | collective-permute-done | bytes 524320 | tf_op jit(solution)/shard_map/ppermute | solution.py:787
  142.1 1.7 %collective-permute-done.34.fb = bf16[64,4096]{1,0:T(8,128)(2,1)S(1)} collective-permute-done((bf16[64,4096]{1,0:T(8,128)(2,1)S(1)}, bf16[64,4096]{1,0:T(8,128)(2,1)S(1)}, u32[]{:S(2)}, u32[]{:S(2)}) %collective-permute-start.34) | collective-permute-done | bytes 524320 | tf_op jit(solution)/shard_map/ppermute | solution.py:789
  143.8 3.9 %collective-permute-done.31.fa = bf16[64,4096]{1,0:T(8,128)(2,1)S(1)} collective-permute-done((bf16[64,4096]{1,0:T(8,128)(2,1)S(1)}, bf16[64,4096]{1,0:T(8,128)(2,1)S(1)}, u32[]{:S(2)}, u32[]{:S(2)}) %collective-permute-start.31) | collective-permute-done | bytes 524320 | tf_op jit(solution)/shard_map/ppermute | solution.py:788
  (57 shorter events, 17.1 us)
Async XLA Ops:
  0.7 10.4 %collective-permute-start.2 = (s32[4]{0:T(128)}, s32[4]{0:T(128)S(1)}, u32[]{:S(2)}, u32[]{:S(2)}) collective-permute-start(s32[4]{0:T(128)} %param.28), channel_id=1, source_target_pairs={{0,0},{4,128},{8,4},{12,132},{16,8},{20,136},{24,12},{28,140},{32,... | collective-permute-start | bytes 56 | tf_op jit(solution)/shard_map/ppermute | solution.py:751
  2.6 8.5 %collective-permute-start.3 = (s32[4]{0:T(128)}, s32[4]{0:T(128)S(1)}, u32[]{:S(2)}, u32[]{:S(2)}) collective-permute-start(s32[4]{0:T(128)} %param.28), channel_id=1, source_target_pairs={{0,128},{4,0},{8,132},{12,4},{16,136},{20,8},{24,140},{28,12},{32,... | collective-permute-start | bytes 56 | tf_op jit(solution)/shard_map/ppermute | solution.py:752
  13.4 8.1 %collective-permute-start.7 = (bf16[1040,128]{1,0:T(8,128)(2,1)S(1)}, bf16[1040,128]{1,0:T(8,128)(2,1)S(1)}, u32[]{:S(2)}, u32[]{:S(2)}) collective-permute-start(bf16[1040,128]{1,0:T(8,128)(2,1)S(1)} %get-tuple-element.1043.refs_4_), channel_id=1, source_target_pairs={{0,16},{4,20},{8,24},{12,28},{16,32},{20,36},{24,40},{28,44},{32,4... | collective-permute-start | bytes 798728 | tf_op jit(solution)/shard_map/ppermute | solution.py:142
  15.2 10.3 %collective-permute-start.11 = (bf16[1040,128]{1,0:T(8,128)(2,1)S(1)}, bf16[1040,128]{1,0:T(8,128)(2,1)S(1)}, u32[]{:S(2)}, u32[]{:S(2)}) collective-permute-start(bf16[1040,128]{1,0:T(8,128)(2,1)S(1)} %get-tuple-element.1043.refs_4_), channel_id=1, source_target_pairs={{0,112},{4,116},{8,120},{12,124},{16,0},{20,4},{24,8},{28,12},{32,... | collective-permute-start | bytes 798728 | tf_op jit(solution)/shard_map/ppermute | solution.py:142
  21.5 9.8 %collective-permute-start.8 = (bf16[1040,128]{1,0:T(8,128)(2,1)S(1)}, bf16[1040,128]{1,0:T(8,128)(2,1)S(1)}, u32[]{:S(2)}, u32[]{:S(2)}) collective-permute-start(bf16[1040,128]{1,0:T(8,128)(2,1)S(1)} %collective-permute-done.7.refs_5_), channel_id=1, source_target_pairs={{0,16},{4,20},{8,24},{12,28},{16,32},{20,36},{24,40},{28,44},{32,4... | collective-permute-start | bytes 798728 | tf_op jit(solution)/shard_map/ppermute | solution.py:142
  25.2 10.4 %collective-permute-start.20 = (bf16[1024,128]{1,0:T(8,128)(2,1)S(1)}, bf16[1024,128]{1,0:T(8,128)(2,1)S(1)}, u32[]{:S(2)}, u32[]{:S(2)}) collective-permute-start(bf16[1024,128]{1,0:T(8,128)(2,1)S(1)} %get-tuple-element.1050.refs_0_), channel_id=1, source_target_pairs={{0,112},{4,116},{8,120},{12,124},{16,0},{20,4},{24,8},{28,12},{32,... | collective-permute-start | bytes 786440 | tf_op jit(solution)/shard_map/ppermute | solution.py:142
  25.5 15.8 %collective-permute-start.12 = (bf16[1040,128]{1,0:T(8,128)(2,1)S(1)}, bf16[1040,128]{1,0:T(8,128)(2,1)S(1)}, u32[]{:S(2)}, u32[]{:S(2)}) collective-permute-start(bf16[1040,128]{1,0:T(8,128)(2,1)S(1)} %collective-permute-done.11.refs_11_), channel_id=1, source_target_pairs={{0,112},{4,116},{8,120},{12,124},{16,0},{20,4},{24,8},{28,12},{32,... | collective-permute-start | bytes 798728 | tf_op jit(solution)/shard_map/ppermute | solution.py:142
  31.3 10.5 %collective-permute-start.9 = (bf16[1040,128]{1,0:T(8,128)(2,1)S(1)}, bf16[1040,128]{1,0:T(8,128)(2,1)S(1)}, u32[]{:S(2)}, u32[]{:S(2)}) collective-permute-start(bf16[1040,128]{1,0:T(8,128)(2,1)S(1)} %collective-permute-done.8.refs_6_), channel_id=1, source_target_pairs={{0,16},{4,20},{8,24},{12,28},{16,32},{20,36},{24,40},{28,44},{32,4... | collective-permute-start | bytes 798728 | tf_op jit(solution)/shard_map/ppermute | solution.py:142
  35.0 12.4 %collective-permute-start.17 = (bf16[1024,128]{1,0:T(8,128)(2,1)S(1)}, bf16[1024,128]{1,0:T(8,128)(2,1)S(1)}, u32[]{:S(2)}, u32[]{:S(2)}) collective-permute-start(bf16[1024,128]{1,0:T(8,128)(2,1)S(1)} %get-tuple-element.1050.refs_0_), channel_id=1, source_target_pairs={{0,16},{4,20},{8,24},{12,28},{16,32},{20,36},{24,40},{28,44},{32,4... | collective-permute-start | bytes 786440 | tf_op jit(solution)/shard_map/ppermute | solution.py:142
  35.6 15.5 %collective-permute-start.21 = (bf16[1024,128]{1,0:T(8,128)(2,1)S(1)}, bf16[1024,128]{1,0:T(8,128)(2,1)S(1)}, u32[]{:S(2)}, u32[]{:S(2)}) collective-permute-start(bf16[1024,128]{1,0:T(8,128)(2,1)S(1)} %collective-permute-done.20.refs_7_), channel_id=1, source_target_pairs={{0,112},{4,116},{8,120},{12,124},{16,0},{20,4},{24,8},{28,12},{32,... | collective-permute-start | bytes 786440 | tf_op jit(solution)/shard_map/ppermute | solution.py:142
  41.3 23.3 %collective-permute-start.13 = (bf16[1040,128]{1,0:T(8,128)(2,1)S(1)}, bf16[1040,128]{1,0:T(8,128)(2,1)S(1)}, u32[]{:S(2)}, u32[]{:S(2)}) collective-permute-start(bf16[1040,128]{1,0:T(8,128)(2,1)S(1)} %collective-permute-done.12.refs_10_), channel_id=1, source_target_pairs={{0,112},{4,116},{8,120},{12,124},{16,0},{20,4},{24,8},{28,12},{32,... | collective-permute-start | bytes 798728 | tf_op jit(solution)/shard_map/ppermute | solution.py:142
  41.8 22.9 %collective-permute-start.10 = (bf16[1040,128]{1,0:T(8,128)(2,1)S(1)}, bf16[1040,128]{1,0:T(8,128)(2,1)S(1)}, u32[]{:S(2)}, u32[]{:S(2)}) collective-permute-start(bf16[1040,128]{1,0:T(8,128)(2,1)S(1)} %collective-permute-done.9.refs_7_), channel_id=1, source_target_pairs={{0,16},{4,20},{8,24},{12,28},{16,32},{20,36},{24,40},{28,44},{32,4... | collective-permute-start | bytes 798728 | tf_op jit(solution)/shard_map/ppermute | solution.py:147
  47.4 24.8 %collective-permute-start.18 = (bf16[1024,128]{1,0:T(8,128)(2,1)S(1)}, bf16[1024,128]{1,0:T(8,128)(2,1)S(1)}, u32[]{:S(2)}, u32[]{:S(2)}) collective-permute-start(bf16[1024,128]{1,0:T(8,128)(2,1)S(1)} %collective-permute-done.17.refs_1_), channel_id=1, source_target_pairs={{0,16},{4,20},{8,24},{12,28},{16,32},{20,36},{24,40},{28,44},{32,4... | collective-permute-start | bytes 786440 | tf_op jit(solution)/shard_map/ppermute | solution.py:142
  51.1 24.3 %collective-permute-start.22 = (bf16[1024,128]{1,0:T(8,128)(2,1)S(1)}, bf16[1024,128]{1,0:T(8,128)(2,1)S(1)}, u32[]{:S(2)}, u32[]{:S(2)}) collective-permute-start(bf16[1024,128]{1,0:T(8,128)(2,1)S(1)} %collective-permute-done.21.refs_6_), channel_id=1, source_target_pairs={{0,112},{4,116},{8,120},{12,124},{16,0},{20,4},{24,8},{28,12},{32,... | collective-permute-start | bytes 786440 | tf_op jit(solution)/shard_map/ppermute | solution.py:142
  51.1 4.9 %collective-permute-start.4 = (s32[8]{0:T(128)S(1)}, s32[8]{0:T(128)S(1)}, u32[]{:S(2)}, u32[]{:S(2)}) collective-permute-start(s32[8]{0:T(128)S(1)} %get-tuple-element.1042.refs_0_.list_ref), channel_id=1, source_target_pairs={{0,12},{4,0},{8,4},{12,8},{16,28},{20,16},{24,20},{28,24},{32,44},... | collective-permute-start | bytes 104 | tf_op jit(solution)/shard_map/ppermute | solution.py:758
  56.0 5.1 %collective-permute-start.5 = (s32[8]{0:T(128)S(1)}, s32[8]{0:T(128)S(1)}, u32[]{:S(2)}, u32[]{:S(2)}) collective-permute-start(s32[8]{0:T(128)S(1)} %get-tuple-element.1042.refs_0_.list_ref), channel_id=1, source_target_pairs={{0,8},{4,12},{8,0},{12,4},{16,24},{20,28},{24,16},{28,20},{32,40},... | collective-permute-start | bytes 104 | tf_op jit(solution)/shard_map/ppermute | solution.py:758
  70.6 17.6 %collective-permute-start.14 = (bf16[1040,128]{1,0:T(8,128)(2,1)S(1)}, bf16[1040,128]{1,0:T(8,128)(2,1)S(1)}, u32[]{:S(2)}, u32[]{:S(2)}) collective-permute-start(bf16[1040,128]{1,0:T(8,128)(2,1)S(1)} %get-tuple-element.1045), channel_id=1, source_target_pairs={{0,4},{4,8},{8,12},{12,0},{16,20},{20,24},{24,28},{28,16},{32,36},... | collective-permute-start | bytes 798728 | tf_op jit(solution)/shard_map/ppermute | solution.py:768
  72.2 7.1 %collective-permute-start.19 = (bf16[1024,128]{1,0:T(8,128)(2,1)S(1)}, bf16[1024,128]{1,0:T(8,128)(2,1)S(1)}, u32[]{:S(2)}, u32[]{:S(2)}) collective-permute-start(bf16[1024,128]{1,0:T(8,128)(2,1)S(1)} %collective-permute-done.18.refs_2_), channel_id=1, source_target_pairs={{0,16},{4,20},{8,24},{12,28},{16,32},{20,36},{24,40},{28,44},{32,4... | collective-permute-start | bytes 786440 | tf_op jit(solution)/shard_map/ppermute | solution.py:142
  75.4 7.6 %collective-permute-start.23 = (bf16[1024,128]{1,0:T(8,128)(2,1)S(1)}, bf16[1024,128]{1,0:T(8,128)(2,1)S(1)}, u32[]{:S(2)}, u32[]{:S(2)}) collective-permute-start(bf16[1024,128]{1,0:T(8,128)(2,1)S(1)} %collective-permute-done.22.refs_5_), channel_id=1, source_target_pairs={{0,112},{4,116},{8,120},{12,124},{16,0},{20,4},{24,8},{28,12},{32,... | collective-permute-start | bytes 786440 | tf_op jit(solution)/shard_map/ppermute | solution.py:148
  75.4 12.8 %collective-permute-start.15 = (bf16[1040,128]{1,0:T(8,128)(2,1)S(1)}, bf16[1040,128]{1,0:T(8,128)(2,1)S(1)}, u32[]{:S(2)}, u32[]{:S(2)}) collective-permute-start(bf16[1040,128]{1,0:T(8,128)(2,1)S(1)} %get-tuple-element.1046), channel_id=1, source_target_pairs={{0,8},{4,12},{8,0},{12,4},{16,24},{20,28},{24,16},{28,20},{32,40},... | collective-permute-start | bytes 798728 | tf_op jit(solution)/shard_map/ppermute | solution.py:768
  76.4 16.3 %collective-permute-start.16 = (bf16[1040,128]{1,0:T(8,128)(2,1)S(1)}, bf16[1040,128]{1,0:T(8,128)(2,1)S(1)}, u32[]{:S(2)}, u32[]{:S(2)}) collective-permute-start(bf16[1040,128]{1,0:T(8,128)(2,1)S(1)} %get-tuple-element.1047), channel_id=1, source_target_pairs={{0,12},{4,0},{8,4},{12,8},{16,28},{20,16},{24,20},{28,24},{32,44},... | collective-permute-start | bytes 798728 | tf_op jit(solution)/shard_map/ppermute | solution.py:768
  85.6 16.6 %collective-permute-start.24 = (bf16[1024,128]{1,0:T(8,128)(2,1)S(1)}, bf16[1024,128]{1,0:T(8,128)(2,1)S(1)}, u32[]{:S(2)}, u32[]{:S(2)}) collective-permute-start(bf16[1024,128]{1,0:T(8,128)(2,1)S(1)} %get-tuple-element.1052), channel_id=1, source_target_pairs={{0,4},{4,8},{8,12},{12,0},{16,20},{20,24},{24,28},{28,16},{32,36},... | collective-permute-start | bytes 786440 | tf_op jit(solution)/shard_map/ppermute | solution.py:776
  85.7 16.5 %collective-permute-start.25 = (bf16[1024,128]{1,0:T(8,128)(2,1)S(1)}, bf16[1024,128]{1,0:T(8,128)(2,1)S(1)}, u32[]{:S(2)}, u32[]{:S(2)}) collective-permute-start(bf16[1024,128]{1,0:T(8,128)(2,1)S(1)} %get-tuple-element.1053), channel_id=1, source_target_pairs={{0,8},{4,12},{8,0},{12,4},{16,24},{20,28},{24,16},{28,20},{32,40},... | collective-permute-start | bytes 786440 | tf_op jit(solution)/shard_map/ppermute | solution.py:776
  88.2 14.0 %collective-permute-start.26 = (bf16[1024,128]{1,0:T(8,128)(2,1)S(1)}, bf16[1024,128]{1,0:T(8,128)(2,1)S(1)}, u32[]{:S(2)}, u32[]{:S(2)}) collective-permute-start(bf16[1024,128]{1,0:T(8,128)(2,1)S(1)} %get-tuple-element.1054), channel_id=1, source_target_pairs={{0,12},{4,0},{8,4},{12,8},{16,28},{20,16},{24,20},{28,24},{32,44},... | collective-permute-start | bytes 786440 | tf_op jit(solution)/shard_map/ppermute | solution.py:776
  116.2 9.8 %collective-permute-start.33 = (bf16[64,2048]{1,0:T(8,128)(2,1)S(1)}, bf16[64,2048]{1,0:T(8,128)(2,1)S(1)}, u32[]{:S(2)}, u32[]{:S(2)}) collective-permute-start(bf16[64,2048]{1,0:T(8,128)(2,1)S(1)} %get-tuple-element.1072), channel_id=1, source_target_pairs={{0,3},{1,0},{2,1},{3,2},{4,7},{5,4},{6,5},{7,6},{8,11},{9,8},{10,9... | collective-permute-start | bytes 786440 | tf_op jit(solution)/shard_map/ppermute | solution.py:785
  119.3 12.3 %collective-permute-start.32 = (bf16[64,2048]{1,0:T(8,128)(2,1)S(1)}, bf16[64,2048]{1,0:T(8,128)(2,1)S(1)}, u32[]{:S(2)}, u32[]{:S(2)}) collective-permute-start(bf16[64,2048]{1,0:T(8,128)(2,1)S(1)} %get-tuple-element.1071), channel_id=1, source_target_pairs={{0,3},{1,0},{2,1},{3,2},{4,7},{5,4},{6,5},{7,6},{8,11},{9,8},{10,9... | collective-permute-start | bytes 786440 | tf_op jit(solution)/shard_map/ppermute | solution.py:782
  120.1 15.5 %collective-permute-start.30 = (bf16[64,2048]{1,0:T(8,128)(2,1)S(1)}, bf16[64,2048]{1,0:T(8,128)(2,1)S(1)}, u32[]{:S(2)}, u32[]{:S(2)}) collective-permute-start(bf16[64,2048]{1,0:T(8,128)(2,1)S(1)} %get-tuple-element.1069), channel_id=1, source_target_pairs={{0,1},{1,2},{2,3},{3,0},{4,5},{5,6},{6,7},{7,4},{8,9},{9,10},{10,1... | collective-permute-start | bytes 786440 | tf_op jit(solution)/shard_map/ppermute | solution.py:784
  121.3 14.7 %collective-permute-start.29 = (bf16[64,2048]{1,0:T(8,128)(2,1)S(1)}, bf16[64,2048]{1,0:T(8,128)(2,1)S(1)}, u32[]{:S(2)}, u32[]{:S(2)}) collective-permute-start(bf16[64,2048]{1,0:T(8,128)(2,1)S(1)} %get-tuple-element.1068), channel_id=1, source_target_pairs={{0,1},{1,2},{2,3},{3,0},{4,5},{5,6},{6,7},{7,4},{8,9},{9,10},{10,1... | collective-permute-start | bytes 786440 | tf_op jit(solution)/shard_map/ppermute | solution.py:781
  121.4 16.8 %collective-permute-start.27 = (bf16[64,4096]{1,0:T(8,128)(2,1)S(1)}, bf16[64,4096]{1,0:T(8,128)(2,1)S(1)}, u32[]{:S(2)}, u32[]{:S(2)}) collective-permute-start(bf16[64,4096]{1,0:T(8,128)(2,1)S(1)} %get-tuple-element.1065), channel_id=1, source_target_pairs={{0,3},{1,0},{2,1},{3,2},{4,7},{5,4},{6,5},{7,6},{8,11},{9,8},{10,9... | collective-permute-start | bytes 1572872 | tf_op jit(solution)/shard_map/ppermute | solution.py:786
  126.0 16.1 %collective-permute-start.28 = (bf16[64,4096]{1,0:T(8,128)(2,1)S(1)}, bf16[64,4096]{1,0:T(8,128)(2,1)S(1)}, u32[]{:S(2)}, u32[]{:S(2)}) collective-permute-start(bf16[64,4096]{1,0:T(8,128)(2,1)S(1)} %get-tuple-element.1066), channel_id=1, source_target_pairs={{0,1},{1,2},{2,3},{3,0},{4,5},{5,6},{6,7},{7,4},{8,9},{9,10},{10,1... | collective-permute-start | bytes 1572872 | tf_op jit(solution)/shard_map/ppermute | solution.py:787
  131.7 12.1 %collective-permute-start.34 = (bf16[64,4096]{1,0:T(8,128)(2,1)S(1)}, bf16[64,4096]{1,0:T(8,128)(2,1)S(1)}, u32[]{:S(2)}, u32[]{:S(2)}) collective-permute-start(bf16[64,4096]{1,0:T(8,128)(2,1)S(1)} %combine.3), channel_id=1, source_target_pairs={{0,3},{1,0},{2,1},{3,2},{4,7},{5,4},{6,5},{7,6},{8,11},{9,8},{10,9... | collective-permute-start | bytes 1572872 | tf_op jit(solution)/shard_map/ppermute | solution.py:789
  136.2 11.5 %collective-permute-start.31 = (bf16[64,4096]{1,0:T(8,128)(2,1)S(1)}, bf16[64,4096]{1,0:T(8,128)(2,1)S(1)}, u32[]{:S(2)}, u32[]{:S(2)}) collective-permute-start(bf16[64,4096]{1,0:T(8,128)(2,1)S(1)} %combine.2), channel_id=1, source_target_pairs={{0,1},{1,2},{2,3},{3,0},{4,5},{5,6},{6,7},{7,4},{8,9},{9,10},{10,1... | collective-permute-start | bytes 1572872 | tf_op jit(solution)/shard_map/ppermute | solution.py:788
  (6 other events, 211.5 us)
where the time goes:
time: 150 us; the launch traced here: 149 us
  waiting for transfers between devices  66.5 us (44%)
  starting transfers between devices  44.4 us (30%)
  Pallas kernels  36 us (24%)
    ppermute x6, waiting for transfers between devices, ring_step(): lax.ppermute(up, 'slot', zperm(1))  17.1 us
    ppermute x6, starting transfers between devices, ring_step(): lax.ppermute(up, 'slot', zperm(1))  16 us
    ppermute x3, waiting for transfers between devices, shards(): lists.append(lax.ppermute(own_list, 'slot', xperm(-d)))  11.1 us
    pallas_call x1, Pallas kernels, early(): pl.pallas_call(functools.partial(early_body, float(dim) ** (-0.5)), out_s...  9.46 us
    ppermute x1, waiting for transfers between devices, shards(): mine = lax.ppermute(fork_src, ('role', 'slot'), halves_perm(0, n_slot))  8.29 us
    pallas_call x1, Pallas kernels, late(): pl.pallas_call(functools.partial(late_body, float(shape[3]) ** (-0.5), ti...  8.27 us
    pallas_call x1, Pallas kernels, select_first(): pl.pallas_call(select_first_body, out_shape=(out,) * NX + (jax.ShapeDtype...  5.97 us
    pallas_call x1, Pallas kernels, project(): pl.pallas_call(functools.partial(project_body, tile), out_shape=(wide, sl...  5.73 us
  transfers between devices with their start and end apart: 33, of which 21 were waited for; matrix products, arithmetic and copies ran while one was open for 0% of the time, Pallas kernels for 12%

commit v1 on v0

--- a/solution.py
+++ b/solution.py
@@ -152,7 +152,7 @@
     return [own, one[0], two[0], three[0], last, three[1], two[1], one[1]]
 
 
-def issue_units(pick_ref, srcs, outs, size, sems):
+def copy_units(pick_ref, srcs, outs, size):
     for d in range(NX):
 
         def unit(i, carry, d=d):
@@ -166,48 +166,33 @@
                     for kv in range(2):
                         at = pl.multiple_of((kv * 2 + rank) * size, META)
                         to = pl.multiple_of((kv * 2 + i) * size, META)
-                        pltpu.make_async_copy(
-                            srcs[r].at[pl.ds(at, size), :],
-                            outs[d].at[pl.ds(to, size), :],
-                            sems.at[u * 2 + kv],
-                        ).start()
+                        outs[d][pl.ds(to, size), :] = srcs[r][pl.ds(at, size), :]
 
             return carry
 
         lax.fori_loop(0, FAST, unit, 0)
 
 
-def wait_units(srcs, outs, size, sems):
-    def unit(n, carry):
-        pltpu.make_async_copy(
-            srcs[0].at[pl.ds(0, size), :], outs[0].at[pl.ds(0, size), :], sems.at[n]
-        ).wait()
-        return carry
-
-    lax.fori_loop(0, NX * FAST * 2, unit, 0)
+def spill(tiles, wide_ref, ids_ref, sem):
+    for i, tile in enumerate(tiles):
+        row = jnp.max(tile.astype(jnp.float32), axis=0, keepdims=True)
+        wide_ref[i : i + 1, :] = row.astype(jnp.int32)
+    copy = pltpu.make_async_copy(wide_ref, ids_ref, sem)
+    copy.start()
+    copy.wait()
 
 
 def select_first_body(where_ref, *refs):
     lists = refs[:NX]
     srcs = refs[NX : NX + NZ]
     outs = refs[NX + NZ : 2 * NX + NZ]
-    pick_ref, meta_ref, wide_ref, ids_ref, sems, msem, ssem = refs[2 * NX + NZ :]
+    pick_ref, wide_ref, ids_ref, sem = refs[2 * NX + NZ :]
     size = outs[0].shape[0] // 4 // META * META
     here = where_ref[1]
     row = here // NX
     col = here % NX
-    reads = []
-    for rel in range(NZ):
-        tile = srcs[rel].at[pl.ds(4 * size, META), :]
-        reads.append(pltpu.make_async_copy(tile, meta_ref.at[rel], msem.at[rel]))
-    for c in reads:
-        c.start()
-    for c in reads:
-        c.wait()
-    wide_ref[...] = meta_ref[...].astype(jnp.float32).astype(jnp.int32)
-    spill = pltpu.make_async_copy(wide_ref, ids_ref, ssem)
-    spill.start()
-    spill.wait()
+    tiles = [src[4 * size : 4 * size + META, :] for src in srcs]
+    spill(tiles, wide_ref, ids_ref, sem)
     for u in range(2 * NX * FAST):
         pick_ref[u] = 0
     for d in range(NX):
@@ -223,24 +208,23 @@
             def _():
                 pick_ref[d * FAST + count] = rel
                 pick_ref[NX * FAST + d * FAST + count] = (
-                    parent % NODE == ids_ref[rel, 0, 1]
+                    parent % NODE == ids_ref[rel, 1]
                 ).astype(jnp.int32)
 
             return count + hit.astype(jnp.int32)
 
         lax.fori_loop(0, NODE, scan, jnp.int32(0))
 
-    issue_units(pick_ref, srcs, outs, size, sems)
-    fit = ids_ref[0, 0, 4]
+    copy_units(pick_ref, srcs, outs, size)
+    fit = ids_ref[0, 4]
     for rel in range(1, NZ):
-        fit = jnp.minimum(fit, ids_ref[rel, 0, 4])
+        fit = jnp.minimum(fit, ids_ref[rel, 4])
     for d in range(NX):
         sizes = []
         for i in range(FAST):
             u = d * FAST + i
-            sizes.append(ids_ref[pick_ref[u], 0, 2 + pick_ref[NX * FAST + u]])
+            sizes.append(ids_ref[pick_ref[u], 2 + pick_ref[NX * FAST + u]])
         outs[d][4 * size : 4 * size + META, :] = lane_row((sizes[0], sizes[1], fit))
-    wait_units(srcs, outs, size, sems)
 
 
 def select_first(where, lists, srcs):
@@ -249,14 +233,11 @@
     return pl.pallas_call(
         select_first_body,
         out_shape=(out,) * NX + (jax.ShapeDtypeStruct((2 * NX * FAST,), jnp.int32),),
-        in_specs=[SMEM] * (1 + NX) + [ANY] * NZ,
+        in_specs=[SMEM] * (1 + NX) + [VMEM] * NZ,
         out_specs=(VMEM,) * NX + (SMEM,),
         scratch_shapes=[
-            pltpu.VMEM((NZ, META, 128), own.dtype),
-            pltpu.VMEM((NZ, META, 128), jnp.int32),
-            pltpu.SMEM((NZ, META, 128), jnp.int32),
-            pltpu.SemaphoreType.DMA((NX * FAST * 2,)),
-            pltpu.SemaphoreType.DMA((NZ,)),
+            pltpu.VMEM((NZ, 128), jnp.int32),
+            pltpu.SMEM((NZ, 128), jnp.int32),
             pltpu.SemaphoreType.DMA,
         ],
         compiler_params=params(2),
@@ -265,13 +246,7 @@
 
 
 def select_second_body(pick_ref, *refs):
-    srcs = refs[:NZ]
-    outs = refs[NZ : NZ + NX]
-    sems = refs[NZ + NX]
-    size = outs[0].shape[0] // 4
-
-    issue_units(pick_ref, srcs, outs, size, sems)
-    wait_units(srcs, outs, size, sems)
+    copy_units(pick_ref, refs[:NZ], refs[NZ:], refs[NZ].shape[0] // 4)
 
 
 def select_second(picks, srcs):
@@ -280,9 +255,8 @@
     return pl.pallas_call(
         select_second_body,
         out_shape=(out,) * NX,
-        in_specs=[SMEM] + [ANY] * NZ,
+        in_specs=[SMEM] + [VMEM] * NZ,
         out_specs=(VMEM,) * NX,
-        scratch_shapes=[pltpu.SemaphoreType.DMA((NX * FAST * 2,))],
         compiler_params=params(2),
         name="select_second",
     )(picks, *srcs)
@@ -340,32 +314,48 @@
             ]
 
 
-def moved_copy(src, kv, rank, h, heads, j, b, buf, sem):
-    at = pl.multiple_of(((kv * 2 + rank) * heads + h) * BLK, BLK)
-    return pltpu.make_async_copy(
-        src.at[pl.ds(at, BLK), :], buf.at[j, h, pl.ds(b * BLK, BLK), :], sem
-    )
-
-
-def early_body(scale, where_ref, list_ref, blocks_ref, q_ref, nk_ref, nv_ref, *refs):
+def cache_copies(src, j, bufs, sems):
+    heads = bufs[0].shape[1]
+    return [
+        pltpu.make_async_copy(src[kv].at[j, h], bufs[kv].at[j, h], sems.at[j, kv * heads + h])
+        for kv in range(2)
+        for h in range(heads)
+    ]
+
+
+def moved_copies(blocks, rank, j, bufs, sems):
+    heads = bufs[0].shape[1]
+    copies = []
+    for b, src in enumerate(blocks):
+        for kv in range(2):
+            for h in range(heads):
+                at = pl.multiple_of(((kv * 2 + rank) * heads + h) * BLK, BLK)
+                copies.append(
+                    pltpu.make_async_copy(
+                        src.at[pl.ds(at, BLK), :],
+                        bufs[kv].at[j, h, pl.ds(b * BLK, BLK), :],
+                        sems.at[j, len(copies)],
+                    )
+                )
+    return copies
+
+
+def each_node(body):
+    def step(n, carry):
+        body(n)
+        return carry
+
+    lax.fori_loop(0, NODE, step, 0)
+
+
+def local_body(scale, where_ref, list_ref, blocks_ref, q_ref, nk_ref, nv_ref, *refs):
     caches = refs[0:2]
-    moved = refs[2 : 2 + NX]
-    w_ref, att_ref, w0_ref, table_ref = refs[2 + NX : 6 + NX]
-    kbuf, vbuf, meta_ref, wide_ref, ids_ref, sems, wsem, msem, ssem = refs[6 + NX :]
+    moved = refs[2:4]
+    w_ref, att_ref, w0_ref, table_ref, kbuf, vbuf, wide_ref, ids_ref, sems, sem, wsem = refs[4:]
     bufs = (kbuf, vbuf)
-    heads = kbuf.shape[1]
     here = where_ref[1]
     tp = where_ref[2]
     col = here % NX
-    half = w0_ref.shape[1]
-    reads = []
-    for d in range(NX):
-        at = moved[d].shape[0] - META
-        reads.append(
-            pltpu.make_async_copy(moved[d].at[pl.ds(at, META), :], meta_ref.at[d], msem.at[d])
-        )
-    for c in reads:
-        c.start()
 
     def place(j, counts):
         parent = list_ref[j]
@@ -383,106 +373,153 @@
 
         @pl.when(dist == NX)
         def _():
-            for kv in range(2):
-                pltpu.make_async_copy(caches[kv].at[j], bufs[kv].at[j], sems.at[j, kv]).start()
-
-        for d in range(NX):
-
-            @pl.when(dist == d)
-            def _(d=d):
-                for kv in range(2):
-                    for h in range(heads):
-                        moved_copy(
-                            moved[d], kv, rank, h, heads, j, 0, bufs[kv], sems.at[j, kv * heads + h]
-                        ).start()
+            for c in cache_copies(caches, j, bufs, sems):
+                c.start()
+
+        @pl.when(dist == 0)
+        def _():
+            for c in moved_copies(moved, rank, j, bufs, sems):
+                c.start()
 
         return tuple(after)
 
     lax.fori_loop(0, NODE, place, (jnp.int32(0),) * NX)
-    load = pltpu.make_async_copy(w_ref.at[:, pl.ds(0, half)], w0_ref, wsem)
+    load = pltpu.make_async_copy(w_ref.at[:, pl.ds(0, w0_ref.shape[1])], w0_ref, wsem)
     load.start()
-    for c in reads:
-        c.wait()
-    wide_ref[...] = meta_ref[...].astype(jnp.float32).astype(jnp.int32)
-    spill = pltpu.make_async_copy(wide_ref, ids_ref, ssem)
-    spill.start()
-    spill.wait()
-    fit = ids_ref[0, 0, FAST]
-    for d in range(1, NX):
-        fit = jnp.minimum(fit, ids_ref[d, 0, FAST])
+    rows = moved[0].shape[0]
+    spill([moved[0][rows - META :, :]], wide_ref, ids_ref, sem)
     for i in range(T_FIT, T_SIZE):
-        table_ref[i] = fit
-
-    def measure(j, carry):
-        dist = table_ref[T_FROM + j]
-        from_peer = ids_ref[jnp.minimum(dist, NX - 1), 0, table_ref[T_RANK + j]]
-        table_ref[T_LEN + j] = jnp.where(dist == NX, blocks_ref[j], from_peer)
-        return carry
-
-    lax.fori_loop(0, NODE, measure, 0)
-
-    def node(n, carry):
-        local = table_ref[T_FROM + n] == NX
-        blocks = table_ref[T_LEN + n]
+        table_ref[i] = ids_ref[0, FAST]
+
+    def node(n):
+        dist = table_ref[T_FROM + n]
+        blocks = jnp.where(dist == NX, blocks_ref[n], ids_ref[0, table_ref[T_RANK + n]])
+        table_ref[T_LEN + n] = blocks
+        mine = (dist == NX) | (dist == 0)
         run = functools.partial(
             attend_node, n, scale=scale, tp=tp, q_ref=q_ref, nk_ref=nk_ref, nv_ref=nv_ref,
             kbuf=kbuf, vbuf=vbuf, att_ref=att_ref,
         )
 
-        @pl.when(local)
+        @pl.when(dist == NX)
         def _():
-            for kv in range(2):
-                pltpu.make_async_copy(caches[kv].at[n], bufs[kv].at[n], sems.at[n, kv]).wait()
-
-        @pl.when(jnp.logical_not(local))
+            for c in cache_copies(caches, n, bufs, sems):
+                c.wait()
+
+        @pl.when(dist == 0)
         def _():
-            for kv in range(2):
-                for h in range(heads):
-                    moved_copy(
-                        moved[0], kv, 0, h, heads, n, 0, bufs[kv], sems.at[n, kv * heads + h]
-                    ).wait()
-
-        @pl.when(local & (blocks == 2))
+            for c in moved_copies(moved, 0, n, bufs, sems):
+                c.wait()
+
+        @pl.when(mine & (blocks == 2))
         def _():
             run(tokens=2 * BLK)
 
-        @pl.when(blocks == 1)
+        @pl.when(mine & (blocks == 1))
         def _():
             run(tokens=BLK)
 
-        return carry
-
-    lax.fori_loop(0, NODE, node, 0)
+    each_node(node)
     load.wait()
 
 
-def early(where, own_list, blocks, queries, new_keys, new_values, keys, values, moved, weight):
-    dim = keys.shape[3]
-    inner, cols = weight.shape
-    half = pltpu.VMEM((inner, cols // 2), weight.dtype)
+def half_weight(weight):
+    return pltpu.VMEM((weight.shape[0], weight.shape[1] // 2), weight.dtype)
+
+
+def node_scratch(keys, per_node):
+    return [
+        pltpu.VMEM(keys.shape, keys.dtype),
+        pltpu.VMEM(keys.shape, keys.dtype),
+        pltpu.VMEM((NX, 128), jnp.int32),
+        pltpu.SMEM((NX, 128), jnp.int32),
+        pltpu.SemaphoreType.DMA((NODE, per_node)),
+        pltpu.SemaphoreType.DMA,
+        pltpu.SemaphoreType.DMA,
+    ]
+
+
+def local(where, own_list, blocks, queries, new_keys, new_values, keys, values, moved, weight):
     return pl.pallas_call(
-        functools.partial(early_body, float(dim) ** -0.5),
+        functools.partial(local_body, float(keys.shape[3]) ** -0.5),
         out_shape=(
             pltpu.VMEM(queries.shape, queries.dtype),
-            half,
+            half_weight(weight),
             jax.ShapeDtypeStruct((T_SIZE,), jnp.int32),
         ),
-        in_specs=[SMEM, SMEM, SMEM, VMEM, VMEM, VMEM] + [ANY] * (3 + NX),
+        in_specs=[SMEM, SMEM, SMEM, VMEM, VMEM, VMEM, ANY, ANY, VMEM, VMEM, ANY],
         out_specs=(VMEM, VMEM, SMEM),
-        scratch_shapes=[
-            pltpu.VMEM(keys.shape, keys.dtype),
-            pltpu.VMEM(keys.shape, keys.dtype),
-            pltpu.VMEM((NX, META, 128), keys.dtype),
-            pltpu.VMEM((NX, META, 128), jnp.int32),
-            pltpu.SMEM((NX, META, 128), jnp.int32),
-            pltpu.SemaphoreType.DMA((NODE, 2 * keys.shape[1])),
-            pltpu.SemaphoreType.DMA,
-            pltpu.SemaphoreType.DMA((NX,)),
-            pltpu.SemaphoreType.DMA,
-        ],
+        scratch_shapes=node_scratch(keys, 4 * keys.shape[1]),
+        compiler_params=params(8),
+        name="local",
+    )(where, own_list, blocks, queries, new_keys, new_values, keys, values, *moved, weight)
+
+
+def early_body(scale, where_ref, old_table, q_ref, nk_ref, nv_ref, *refs):
+    moved = refs[: NX - 1]
+    refs = refs[NX - 1 :]
+    w_ref, old_ref, att_ref, w1_ref, table_ref, kbuf, vbuf, wide_ref, ids_ref, sems, sem, wsem = refs
+    del old_ref
+    bufs = (kbuf, vbuf)
+
+    def start(n):
+        for d in range(1, NX):
+
+            @pl.when(old_table[T_FROM + n] == d)
+            def _(d=d):
+                for c in moved_copies(moved[d - 1 : d], old_table[T_RANK + n], n, bufs, sems):
+                    c.start()
+
+    each_node(start)
+    half = w1_ref.shape[1]
+    load = pltpu.make_async_copy(w_ref.at[:, pl.ds(half, half)], w1_ref, wsem)
+    load.start()
+    spill([m[m.shape[0] - META :, :] for m in moved], wide_ref, ids_ref, sem)
+    for i in range(T_LEN):
+        table_ref[i] = old_table[i]
+    fit = old_table[T_FIT]
+    for d in range(1, NX):
+        fit = jnp.minimum(fit, ids_ref[d - 1, FAST])
+    for i in range(T_FIT, T_SIZE):
+        table_ref[i] = fit
+
+    def node(n):
+        dist = old_table[T_FROM + n]
+        far = (dist > 0) & (dist < NX)
+        at = jnp.clip(dist - 1, 0, NX - 2)
+        blocks = jnp.where(far, ids_ref[at, old_table[T_RANK + n]], old_table[T_LEN + n])
+        table_ref[T_LEN + n] = blocks
+
+        @pl.when(far)
+        def _():
+            for c in moved_copies(moved[:1], 0, n, bufs, sems):
+                c.wait()
+
+        @pl.when(far & (blocks == 1))
+        def _():
+            attend_node(
+                n, BLK, scale, where_ref[2], q_ref, nk_ref, nv_ref, kbuf, vbuf, att_ref
+            )
+
+    each_node(node)
+    load.wait()
+
+
+def early(where, table, queries, new_keys, new_values, moved, weight, att, keys):
+    return pl.pallas_call(
+        functools.partial(early_body, float(keys.shape[3]) ** -0.5),
+        out_shape=(
+            pltpu.VMEM(queries.shape, queries.dtype),
+            half_weight(weight),
+            jax.ShapeDtypeStruct((T_SIZE,), jnp.int32),
+        ),
+        in_specs=[SMEM, SMEM, VMEM, VMEM, VMEM] + [VMEM] * (NX - 1) + [ANY, VMEM],
+        out_specs=(VMEM, VMEM, SMEM),
+        scratch_shapes=node_scratch(keys, 2 * keys.shape[1]),
+        input_output_aliases={5 + NX: 0},
         compiler_params=params(8),
         name="early",
-    )(where, own_list, blocks, queries, new_keys, new_values, keys, values, *moved, weight)
+    )(where, table, queries, new_keys, new_values, *moved, weight, att)
 
 
 def project_half(chunk, tile, att_ref, w_ref, own_ref, relay_a, relay_b, da, db, ca, cb):
@@ -506,79 +543,64 @@
 
 
 def late_body(scale, tile, where_ref, table_ref, q_ref, nk_ref, nv_ref, *refs):
-    firsts = refs[:NX]
-    seconds = refs[NX : 2 * NX]
-    old_ref, w0_ref, w_ref, att_ref, w1_ref = refs[2 * NX : 2 * NX + 5]
-    outs = refs[2 * NX + 5 : 2 * NX + 12]
-    kbuf, vbuf, sems, wsem = refs[2 * NX + 12 :]
+    far = NX - 1
+    firsts = refs[:far]
+    seconds = refs[far : 2 * far]
+    old_ref, w_ref, att_ref = refs[2 * far : 2 * far + 3]
+    outs = refs[2 * far + 3 : 2 * far + 10]
+    kbuf, vbuf, sems = refs[2 * far + 10 :]
     del old_ref
     bufs = (kbuf, vbuf)
-    heads = kbuf.shape[1]
-    tp = where_ref[2]
-    half = w1_ref.shape[1]
 
     def is_late(n):
-        return (table_ref[T_FROM + n] < NX) & (table_ref[T_LEN + n] == 2)
-
-    def copies(n, d, rank):
-        for b, group in enumerate((firsts, seconds)):
-            for kv in range(2):
-                for h in range(heads):
-                    yield moved_copy(
-                        group[d], kv, rank, h, heads, n, b, bufs[kv],
-                        sems.at[n, (b * 2 + kv) * heads + h],
-                    )
-
-    def start(n, carry):
-        for d in range(NX):
+        dist = table_ref[T_FROM + n]
+        return (dist > 0) & (dist < NX) & (table_ref[T_LEN + n] == 2)
+
+    def start(n):
+        for d in range(1, NX):
 
             @pl.when(is_late(n) & (table_ref[T_FROM + n] == d))
             def _(d=d):
-                for c in copies(n, d, table_ref[T_RANK + n]):
+                pair = (firsts[d - 1], seconds[d - 1])
+                for c in moved_copies(pair, table_ref[T_RANK + n], n, bufs, sems):
                     c.start()
 
-        return carry
-
-    lax.fori_loop(0, NODE, start, 0)
-    load = pltpu.make_async_copy(w_ref.at[:, pl.ds(half, half)], w1_ref, wsem)
-    load.start()
-
-    def node(n, carry):
+    each_node(start)
+
+    def node(n):
         @pl.when(is_late(n))
         def _():
-            for c in copies(n, 0, 0):
+            for c in moved_copies((firsts[0], seconds[0]), 0, n, bufs, sems):
                 c.wait()
-            attend_node(n, 2 * BLK, scale, tp, q_ref, nk_ref, nv_ref, kbuf, vbuf, att_ref)
-
-        return carry
-
-    lax.fori_loop(0, NODE, node, 0)
-    project_half(0, tile, att_ref, w0_ref, *outs)
-    load.wait()
-
-
-def late(where, table, queries, new_keys, new_values, moved, att, weight0, weight, shape, tile):
+            attend_node(
+                n, 2 * BLK, scale, where_ref[2], q_ref, nk_ref, nv_ref, kbuf, vbuf, att_ref
+            )
+
+    each_node(node)
+    project_half(0, tile, att_ref, w_ref, *outs)
+
+
+def late(where, table, queries, new_keys, new_values, firsts, seconds, att, weight0, shape, tile):
     dtype = queries.dtype
     part = att.shape[0] // NTP
-    inner, half = weight0.shape
+    half = weight0.shape[1]
     wide = pltpu.VMEM((part, half), dtype)
     slim = pltpu.VMEM((part, half // 2), dtype)
+    far = NX - 1
     return pl.pallas_call(
         functools.partial(late_body, float(shape[3]) ** -0.5, tile),
-        out_shape=(pltpu.VMEM(att.shape, dtype), pltpu.VMEM((inner, half), dtype))
-        + (wide, slim, slim, wide, wide, wide, wide),
-        in_specs=[SMEM, SMEM, VMEM, VMEM, VMEM] + [ANY] * (2 * NX) + [VMEM, VMEM, ANY],
-        out_specs=(VMEM,) * 9,
+        out_shape=(pltpu.VMEM(att.shape, dtype), wide, slim, slim, wide, wide, wide, wide),
+        in_specs=[SMEM, SMEM, VMEM, VMEM, VMEM] + [ANY] * (2 * far) + [VMEM, VMEM],
+        out_specs=(VMEM,) * 8,
         scratch_shapes=[
             pltpu.VMEM(shape, dtype),
             pltpu.VMEM(shape, dtype),
             pltpu.SemaphoreType.DMA((NODE, 4 * shape[1])),
-            pltpu.SemaphoreType.DMA,
         ],
-        input_output_aliases={5 + 2 * NX: 0},
+        input_output_aliases={5 + 2 * far: 0},
         compiler_params=params(8),
         name="late",
-    )(where, table, queries, new_keys, new_values, *moved, att, weight0, weight)
+    )(where, table, queries, new_keys, new_values, *firsts, *seconds, att, weight0)
 
 
 def project_body(tile, att_ref, w_ref, da0, db0, ca0, cb0, own_ref, ra, rb, da, db, ca, cb):
@@ -763,19 +785,22 @@
     got_first = ring_list(first, first1, first2, first3, ring_last(first3, True))
     got_second = ring_list(second, second1, second2, second3, ring_last(second3, False))
     *outs_first, picks = select_first(where, lists, got_first)
-    moved = [outs_first[0]]
+    firsts = []
     for d in (1, 2, 3):
-        moved.append(lax.ppermute(outs_first[d], "slot", xperm(d)))
+        firsts.append(lax.ppermute(outs_first[d], "slot", xperm(d)))
     outs_second = select_second(picks, got_second)
-    att, weight0, table = early(
-        where, own_list, cache_blocks, queries, new_keys, new_values, keys, values, moved,
-        weight,
+    seconds = []
+    for d in (1, 2, 3):
+        seconds.append(lax.ppermute(outs_second[d], "slot", xperm(d)))
+    att, weight0, table = local(
+        where, own_list, cache_blocks, queries, new_keys, new_values, keys, values,
+        (outs_first[0], outs_second[0]), weight,
     )
-    moved = moved + [outs_second[0]]
-    for d in (1, 2, 3):
-        moved.append(lax.ppermute(outs_second[d], "slot", xperm(d)))
-    att, weight1, own0, relay_a0, relay_b0, *shared = late(
-        where, table, queries, new_keys, new_values, moved, att, weight0, weight, keys.shape, 512
+    att, weight1, table = early(
+        where, table, queries, new_keys, new_values, firsts, weight, att, keys
+    )
+    att, own0, relay_a0, relay_b0, *shared = late(
+        where, table, queries, new_keys, new_values, firsts, seconds, att, weight0, keys.shape, 512
     )
     up, down = yperm(1), yperm(-1)
     relay_a0 = lax.ppermute(relay_a0, "tp", up)

time: 150 us -> 153 us (1.020); the launches traced: 149 us -> 150 us
  Pallas kernels: 36 us -> 39.6 us
  waiting for transfers between devices: 66.5 us -> 63.7 us
    pallas_call x1 -> x2, Pallas kernels: 9.46 us -> 17.4 us  [the longest x1 9.23 us: local(): pl.pallas_call(functools.partial(local_body, float(keys.shape[3]) ** (-0....]
    ppermute x6, waiting for transfers between devices: 4.44 us -> 0.02 us  [the longest x3 0.01 us: shards(): firsts.append(lax.ppermute(outs_first[d], 'slot', xperm(d)))]
    pallas_call x1, Pallas kernels: 5.97 us -> 3.25 us  [select_first(): pl.pallas_call(select_first_body, out_shape=(out,) * NX + (jax.ShapeDtype...]
    ppermute x1, waiting for transfers between devices: 0.61 us -> 2.28 us  [shards(): da = lax.ppermute(da, 'tp', down)]
    pallas_call x1, Pallas kernels: 2.56 us -> 1 us  [select_second(): pl.pallas_call(select_second_body, out_shape=(out,) * NX, in_specs=[SMEM]...]
  transfers between devices with their start and end apart: 33 -> 33, of which waited for: 21 -> 20; matrix products, arithmetic and copies ran while one was open for 0% -> 0% of each run, Pallas kernels for 12% -> 15%
where the time goes in v1:
time: 153 us; the launch traced here: 150 us
  waiting for transfers between devices  63.7 us (42%)
  starting transfers between devices  44.4 us (29%)
  Pallas kernels  39.6 us (26%)
    ppermute x6, waiting for transfers between devices, ring_step(): lax.ppermute(up, 'slot', zperm(1))  17.1 us
    ppermute x6, starting transfers between devices, ring_step(): lax.ppermute(up, 'slot', zperm(1))  16 us
    ppermute x3, waiting for transfers between devices, shards(): lists.append(lax.ppermute(own_list, 'slot', xperm(-d)))  11.1 us
    pallas_call x1, Pallas kernels, local(): pl.pallas_call(functools.partial(local_body, float(keys.shape[3]) ** (-0....  9.23 us
    ppermute x1, waiting for transfers between devices, shards(): mine = lax.ppermute(fork_src, ('role', 'slot'), halves_perm(0, n_slot))  8.29 us
    pallas_call x1, Pallas kernels, late(): pl.pallas_call(functools.partial(late_body, float(shape[3]) ** (-0.5), ti...  8.23 us
    pallas_call x1, Pallas kernels, early(): pl.pallas_call(functools.partial(early_body, float(keys.shape[3]) ** (-0....  8.15 us
    pallas_call x1, Pallas kernels, project(): pl.pallas_call(functools.partial(project_body, tile), out_shape=(wide, sl...  5.76 us
  transfers between devices with their start and end apart: 33, of which 20 were waited for; matrix products, arithmetic and copies ran while one was open for 0% of the time, Pallas kernels for 15%

profile of v1, /device:TPU:102, one launch (start us, length us, event | category | flops | bytes accessed | tf_op | source)
XLA Modules:
  0.0 150.0 jit_solution(7161385732180456949)
XLA Ops:
  0.7 1.9 %collective-permute-start.2 = (s32[4]{0:T(128)}, s32[4]{0:T(128)S(1)}, u32[]{:S(2)}, u32[]{:S(2)}) collective-permute-start(s32[4]{0:T(128)} %param.28), channel_id=1, source_target_pairs={{0,0},{4,128},{8,4},{12,132},{16,8},{20,136},{24,12},{28,140},{32,... | collective-permute-start | bytes 56 | tf_op jit(solution)/shard_map/ppermute | solution.py:773
  2.8 8.3 %collective-permute-done.2.mine_ref = s32[4]{0:T(128)S(1)} collective-permute-done((s32[4]{0:T(128)}, s32[4]{0:T(128)S(1)}, u32[]{:S(2)}, u32[]{:S(2)}) %collective-permute-start.2) | collective-permute-done | bytes 48 | tf_op jit(solution)/shard_map/ppermute | solution.py:773
  11.1 2.4 %pack.3 = (bf16[1040,128]{1,0:T(8,128)(2,1)S(1)}, bf16[1024,128]{1,0:T(8,128)(2,1)S(1)}, s32[8]{0:T(128)S(1)}) custom-call(s32[3]{0:T(128)S(1)} %pad_add_fusion.where_ref, s32[4]{0:T(128)S(1)} %collective-permute-done.2.mine_ref, s32[4]{0:T(128)S(1)} %collective-permute-done.3.other_ref, s32[8]{0:T(128)S(1)} %copy.83.blocks_ref, ...), custom_call_target="tpu_custom_call" | custom-call | tf_op jit(solution)/shard_map/pack/pallas_call | solution.py:125
  13.4 1.7 %collective-permute-start.7 = (bf16[1040,128]{1,0:T(8,128)(2,1)S(1)}, bf16[1040,128]{1,0:T(8,128)(2,1)S(1)}, u32[]{:S(2)}, u32[]{:S(2)}) collective-permute-start(bf16[1040,128]{1,0:T(8,128)(2,1)S(1)} %get-tuple-element.1045.refs_4_), channel_id=1, source_target_pairs={{0,16},{4,20},{8,24},{12,28},{16,32},{20,36},{24,40},{28,44},{32,4... | collective-permute-start | bytes 798728 | tf_op jit(solution)/shard_map/ppermute | solution.py:142
  15.5 6.0 %collective-permute-done.7.refs_5_ = bf16[1040,128]{1,0:T(8,128)(2,1)S(1)} collective-permute-done((bf16[1040,128]{1,0:T(8,128)(2,1)S(1)}, bf16[1040,128]{1,0:T(8,128)(2,1)S(1)}, u32[]{:S(2)}, u32[]{:S(2)}) %collective-permute-start.7) | collective-permute-done | bytes 266272 | tf_op jit(solution)/shard_map/ppermute | solution.py:142
  21.5 3.7 %collective-permute-start.8 = (bf16[1040,128]{1,0:T(8,128)(2,1)S(1)}, bf16[1040,128]{1,0:T(8,128)(2,1)S(1)}, u32[]{:S(2)}, u32[]{:S(2)}) collective-permute-start(bf16[1040,128]{1,0:T(8,128)(2,1)S(1)} %collective-permute-done.7.refs_5_), channel_id=1, source_target_pairs={{0,16},{4,20},{8,24},{12,28},{16,32},{20,36},{24,40},{28,44},{32,4... | collective-permute-start | bytes 798728 | tf_op jit(solution)/shard_map/ppermute | solution.py:142
  25.5 5.8 %collective-permute-done.8.refs_6_ = bf16[1040,128]{1,0:T(8,128)(2,1)S(1)} collective-permute-done((bf16[1040,128]{1,0:T(8,128)(2,1)S(1)}, bf16[1040,128]{1,0:T(8,128)(2,1)S(1)}, u32[]{:S(2)}, u32[]{:S(2)}) %collective-permute-start.8) | collective-permute-done | bytes 266272 | tf_op jit(solution)/shard_map/ppermute | solution.py:142
  31.3 3.7 %collective-permute-start.9 = (bf16[1040,128]{1,0:T(8,128)(2,1)S(1)}, bf16[1040,128]{1,0:T(8,128)(2,1)S(1)}, u32[]{:S(2)}, u32[]{:S(2)}) collective-permute-start(bf16[1040,128]{1,0:T(8,128)(2,1)S(1)} %collective-permute-done.8.refs_6_), channel_id=1, source_target_pairs={{0,16},{4,20},{8,24},{12,28},{16,32},{20,36},{24,40},{28,44},{32,4... | collective-permute-start | bytes 798728 | tf_op jit(solution)/shard_map/ppermute | solution.py:142
  37.0 4.3 %collective-permute-done.12.refs_10_ = bf16[1040,128]{1,0:T(8,128)(2,1)S(1)} collective-permute-done((bf16[1040,128]{1,0:T(8,128)(2,1)S(1)}, bf16[1040,128]{1,0:T(8,128)(2,1)S(1)}, u32[]{:S(2)}, u32[]{:S(2)}) %collective-permute-start.12) | collective-permute-done | bytes 266272 | tf_op jit(solution)/shard_map/ppermute | solution.py:142
  41.8 3.7 %collective-permute-start.10 = (bf16[1040,128]{1,0:T(8,128)(2,1)S(1)}, bf16[1040,128]{1,0:T(8,128)(2,1)S(1)}, u32[]{:S(2)}, u32[]{:S(2)}) collective-permute-start(bf16[1040,128]{1,0:T(8,128)(2,1)S(1)} %collective-permute-done.9.refs_7_), channel_id=1, source_target_pairs={{0,16},{4,20},{8,24},{12,28},{16,32},{20,36},{24,40},{28,44},{32,4... | collective-permute-start | bytes 798728 | tf_op jit(solution)/shard_map/ppermute | solution.py:147
  45.5 1.9 %collective-permute-done.14.refs_1_ = bf16[1024,128]{1,0:T(8,128)(2,1)S(1)} collective-permute-done((bf16[1024,128]{1,0:T(8,128)(2,1)S(1)}, bf16[1024,128]{1,0:T(8,128)(2,1)S(1)}, u32[]{:S(2)}, u32[]{:S(2)}) %collective-permute-start.14) | collective-permute-done | bytes 262176 | tf_op jit(solution)/shard_map/ppermute | solution.py:142
  47.4 3.7 %collective-permute-start.15 = (bf16[1024,128]{1,0:T(8,128)(2,1)S(1)}, bf16[1024,128]{1,0:T(8,128)(2,1)S(1)}, u32[]{:S(2)}, u32[]{:S(2)}) collective-permute-start(bf16[1024,128]{1,0:T(8,128)(2,1)S(1)} %collective-permute-done.14.refs_1_), channel_id=1, source_target_pairs={{0,16},{4,20},{8,24},{12,28},{16,32},{20,36},{24,40},{28,44},{32,4... | collective-permute-start | bytes 786440 | tf_op jit(solution)/shard_map/ppermute | solution.py:142
  52.8 3.2 %collective-permute-done.4.refs_1_ = s32[8]{0:T(128)S(1)} collective-permute-done((s32[8]{0:T(128)S(1)}, s32[8]{0:T(128)S(1)}, u32[]{:S(2)}, u32[]{:S(2)}) %collective-permute-start.4) | collective-permute-done | bytes 64 | tf_op jit(solution)/shard_map/ppermute | solution.py:780
  56.4 4.7 %collective-permute-done.5.refs_2_ = s32[8]{0:T(128)S(1)} collective-permute-done((s32[8]{0:T(128)S(1)}, s32[8]{0:T(128)S(1)}, u32[]{:S(2)}, u32[]{:S(2)}) %collective-permute-start.5) | collective-permute-done | bytes 64 | tf_op jit(solution)/shard_map/ppermute | solution.py:780
  61.3 3.3 %collective-permute-done.6.refs_3_ = s32[8]{0:T(128)S(1)} collective-permute-done((s32[8]{0:T(128)S(1)}, s32[8]{0:T(128)S(1)}, u32[]{:S(2)}, u32[]{:S(2)}) %collective-permute-start.6) | collective-permute-done | bytes 64 | tf_op jit(solution)/shard_map/ppermute | solution.py:780
  64.6 3.2 %select_first.1 = (bf16[1040,128]{1,0:T(8,128)(2,1)S(1)}, bf16[1040,128]{1,0:T(8,128)(2,1)S(1)}, bf16[1040,128]{1,0:T(8,128)(2,1)S(1)}, bf16[1040,128]{1,0:T(8,128)(2,1)S(1)}, s32[16]{0:T(128)S(1)}) custom-call(s32[3]{0:T(128)S(1)} %pad_add_fusion.where_ref, s32[8]{0:T(128)S(1)} %get-tuple-element.1044.refs_0_.list_ref, ...), custom_call_target="tpu_custom_call" | custom-call | tf_op jit(solution)/shard_map/select_first/pallas_call | solution.py:233
  69.5 3.2 %collective-permute-start.16 = (bf16[1024,128]{1,0:T(8,128)(2,1)S(1)}, bf16[1024,128]{1,0:T(8,128)(2,1)S(1)}, u32[]{:S(2)}, u32[]{:S(2)}) collective-permute-start(bf16[1024,128]{1,0:T(8,128)(2,1)S(1)} %collective-permute-done.15.refs_2_), channel_id=1, source_target_pairs={{0,16},{4,20},{8,24},{12,28},{16,32},{20,36},{24,40},{28,44},{32,4... | collective-permute-start | bytes 786440 | tf_op jit(solution)/shard_map/ppermute | solution.py:142
  73.6 2.9 %collective-permute-done.16.refs_3_ = bf16[1024,128]{1,0:T(8,128)(2,1)S(1)} collective-permute-done((bf16[1024,128]{1,0:T(8,128)(2,1)S(1)}, bf16[1024,128]{1,0:T(8,128)(2,1)S(1)}, u32[]{:S(2)}, u32[]{:S(2)}) %collective-permute-start.16) | collective-permute-done | bytes 262176 | tf_op jit(solution)/shard_map/ppermute | solution.py:142
  76.6 3.7 %collective-permute-done.20.refs_4_ = bf16[1024,128]{1,0:T(8,128)(2,1)S(1)} collective-permute-done((bf16[1024,128]{1,0:T(8,128)(2,1)S(1)}, bf16[1024,128]{1,0:T(8,128)(2,1)S(1)}, u32[]{:S(2)}, u32[]{:S(2)}) %collective-permute-start.20) | collective-permute-done | bytes 262176 | tf_op jit(solution)/shard_map/ppermute | solution.py:148
  81.4 2.5 %collective-permute-start.25 = (bf16[1024,128]{1,0:T(8,128)(2,1)S(1)}, bf16[1024,128]{1,0:T(8,128)(2,1)S(1)}, u32[]{:S(2)}, u32[]{:S(2)}) collective-permute-start(bf16[1024,128]{1,0:T(8,128)(2,1)S(1)} %get-tuple-element.1057), channel_id=1, source_target_pairs={{0,8},{4,12},{8,0},{12,4},{16,24},{20,28},{24,16},{28,20},{32,40},... | collective-permute-start | bytes 786440 | tf_op jit(solution)/shard_map/ppermute | solution.py:794
  84.0 9.2 %local.1 = (bf16[256,2048]{1,0:T(8,128)(2,1)S(1)}, bf16[2048,4096]{1,0:T(8,128)(2,1)S(1)}, s32[32]{0:T(128)S(1)}) custom-call(s32[3]{0:T(128)S(1)} %pad_add_fusion.where_ref, s32[8]{0:T(128)S(1)} %get-tuple-element.1044.refs_0_.list_ref, s32[8]{0:T(128)S(1)} %copy.83.blocks_ref, bf16[256,2048]{1,0:T(8,128)(2,1)S(1)} %bitcast.71, ...), custom_call_target="tpu_custom_call" | custom-call | tf_op jit(solution)/shard_map/local/pallas_call | solution.py:443
  93.3 8.2 %early.1 = (bf16[256,2048]{1,0:T(8,128)(2,1)S(1)}, bf16[2048,4096]{1,0:T(8,128)(2,1)S(1)}, s32[32]{0:T(128)S(1)}) custom-call(s32[3]{0:T(128)S(1)} %pad_add_fusion.where_ref, s32[32]{0:T(128)S(1)} %get-tuple-element.1050.old_table, bf16[256,2048]{1,0:T(8,128)(2,1)S(1)} %bitcast.72, bf16[256,256]{1,0:T(8,128)(2,1)S(1)} %bitcast.79, ...), custom_call_target="tpu_custom_call", output_to_operand_aliasing={{0}: (9, {})} | custom-call | tf_op jit(solution)/shard_map/early/pallas_call | solution.py:509
  101.5 8.2 %late.1 = (bf16[256,2048]{1,0:T(8,128)(2,1)S(1)}, bf16[64,4096]{1,0:T(8,128)(2,1)S(1)}, bf16[64,2048]{1,0:T(8,128)(2,1)S(1)}, bf16[64,2048]{1,0:T(8,128)(2,1)S(1...) custom-call(s32[3]{0:T(128)S(1)} %pad_add_fusion.where_ref, ...), custom_call_target="tpu_custom_call", output_to_operand_aliasing={{0}: (11, {})} | custom-call | tf_op jit(solution)/shard_map/late/pallas_call | solution.py:590
  109.7 5.8 %project.1 = (bf16[64,4096]{1,0:T(8,128)(2,1)S(1)}, bf16[64,2048]{1,0:T(8,128)(2,1)S(1)}, bf16[64,2048]{1,0:T(8,128)(2,1)S(1)}, bf16[64,4096]{1,0:T(8,128)(2,1)S...) custom-call(bf16[256,2048]{1,0:T(8,128)(2,1)S(1)} %get-tuple-element, ...), custom_call_target="tpu_custom_call", output_to_operand_aliasing={{3}: (2, {}), {4}: (3, {}), {5}: (4, {}), {6}: (5, {})} | custom-call | tf_op jit(solution)/shard_map/project/pallas_call | solution.py:616
  115.5 3.1 %collective-permute-start.33 = (bf16[64,2048]{1,0:T(8,128)(2,1)S(1)}, bf16[64,2048]{1,0:T(8,128)(2,1)S(1)}, u32[]{:S(2)}, u32[]{:S(2)}) collective-permute-start(bf16[64,2048]{1,0:T(8,128)(2,1)S(1)} %get-tuple-element.1076), channel_id=1, source_target_pairs={{0,3},{1,0},{2,1},{3,2},{4,7},{5,4},{6,5},{7,6},{8,11},{9,8},{10,9... | collective-permute-start | bytes 786440 | tf_op jit(solution)/shard_map/ppermute | solution.py:810
  120.6 3.2 %collective-permute-start.27 = (bf16[64,4096]{1,0:T(8,128)(2,1)S(1)}, bf16[64,4096]{1,0:T(8,128)(2,1)S(1)}, u32[]{:S(2)}, u32[]{:S(2)}) collective-permute-start(bf16[64,4096]{1,0:T(8,128)(2,1)S(1)} %get-tuple-element.1069), channel_id=1, source_target_pairs={{0,3},{1,0},{2,1},{3,2},{4,7},{5,4},{6,5},{7,6},{8,11},{9,8},{10,9... | collective-permute-start | bytes 1572872 | tf_op jit(solution)/shard_map/ppermute | solution.py:811
  126.3 4.6 %collective-permute-done.32.low_ref = bf16[64,2048]{1,0:T(8,128)(2,1)S(1)} collective-permute-done((bf16[64,2048]{1,0:T(8,128)(2,1)S(1)}, bf16[64,2048]{1,0:T(8,128)(2,1)S(1)}, u32[]{:S(2)}, u32[]{:S(2)}) %collective-permute-start.32) | collective-permute-done | bytes 262176 | tf_op jit(solution)/shard_map/ppermute | solution.py:807
  131.0 3.8 %collective-permute-start.34 = (bf16[64,4096]{1,0:T(8,128)(2,1)S(1)}, bf16[64,4096]{1,0:T(8,128)(2,1)S(1)}, u32[]{:S(2)}, u32[]{:S(2)}) collective-permute-start(bf16[64,4096]{1,0:T(8,128)(2,1)S(1)} %combine.3), channel_id=1, source_target_pairs={{0,3},{1,0},{2,1},{3,2},{4,7},{5,4},{6,5},{7,6},{8,11},{9,8},{10,9... | collective-permute-start | bytes 1572872 | tf_op jit(solution)/shard_map/ppermute | solution.py:814
  136.8 2.3 %collective-permute-done.27.da = bf16[64,4096]{1,0:T(8,128)(2,1)S(1)} collective-permute-done((bf16[64,4096]{1,0:T(8,128)(2,1)S(1)}, bf16[64,4096]{1,0:T(8,128)(2,1)S(1)}, u32[]{:S(2)}, u32[]{:S(2)}) %collective-permute-start.27) | collective-permute-done | bytes 524320 | tf_op jit(solution)/shard_map/ppermute | solution.py:811
  139.1 3.9 %collective-permute-done.28.db = bf16[64,4096]{1,0:T(8,128)(2,1)S(1)} collective-permute-done((bf16[64,4096]{1,0:T(8,128)(2,1)S(1)}, bf16[64,4096]{1,0:T(8,128)(2,1)S(1)}, u32[]{:S(2)}, u32[]{:S(2)}) %collective-permute-start.28) | collective-permute-done | bytes 524320 | tf_op jit(solution)/shard_map/ppermute | solution.py:812
  143.0 1.7 %collective-permute-done.34.fb = bf16[64,4096]{1,0:T(8,128)(2,1)S(1)} collective-permute-done((bf16[64,4096]{1,0:T(8,128)(2,1)S(1)}, bf16[64,4096]{1,0:T(8,128)(2,1)S(1)}, u32[]{:S(2)}, u32[]{:S(2)}) %collective-permute-start.34) | collective-permute-done | bytes 524320 | tf_op jit(solution)/shard_map/ppermute | solution.py:814
  144.7 3.9 %collective-permute-done.31.fa = bf16[64,4096]{1,0:T(8,128)(2,1)S(1)} collective-permute-done((bf16[64,4096]{1,0:T(8,128)(2,1)S(1)}, bf16[64,4096]{1,0:T(8,128)(2,1)S(1)}, u32[]{:S(2)}, u32[]{:S(2)}) %collective-permute-start.31) | collective-permute-done | bytes 524320 | tf_op jit(solution)/shard_map/ppermute | solution.py:813
  (58 shorter events, 17.5 us)
Async XLA Ops:
  0.7 10.4 %collective-permute-start.2 = (s32[4]{0:T(128)}, s32[4]{0:T(128)S(1)}, u32[]{:S(2)}, u32[]{:S(2)}) collective-permute-start(s32[4]{0:T(128)} %param.28), channel_id=1, source_target_pairs={{0,0},{4,128},{8,4},{12,132},{16,8},{20,136},{24,12},{28,140},{32,... | collective-permute-start | bytes 56 | tf_op jit(solution)/shard_map/ppermute | solution.py:773
  2.6 8.5 %collective-permute-start.3 = (s32[4]{0:T(128)}, s32[4]{0:T(128)S(1)}, u32[]{:S(2)}, u32[]{:S(2)}) collective-permute-start(s32[4]{0:T(128)} %param.28), channel_id=1, source_target_pairs={{0,128},{4,0},{8,132},{12,4},{16,136},{20,8},{24,140},{28,12},{32,... | collective-permute-start | bytes 56 | tf_op jit(solution)/shard_map/ppermute | solution.py:774
  13.4 8.1 %collective-permute-start.7 = (bf16[1040,128]{1,0:T(8,128)(2,1)S(1)}, bf16[1040,128]{1,0:T(8,128)(2,1)S(1)}, u32[]{:S(2)}, u32[]{:S(2)}) collective-permute-start(bf16[1040,128]{1,0:T(8,128)(2,1)S(1)} %get-tuple-element.1045.refs_4_), channel_id=1, source_target_pairs={{0,16},{4,20},{8,24},{12,28},{16,32},{20,36},{24,40},{28,44},{32,4... | collective-permute-start | bytes 798728 | tf_op jit(solution)/shard_map/ppermute | solution.py:142
  15.2 10.3 %collective-permute-start.11 = (bf16[1040,128]{1,0:T(8,128)(2,1)S(1)}, bf16[1040,128]{1,0:T(8,128)(2,1)S(1)}, u32[]{:S(2)}, u32[]{:S(2)}) collective-permute-start(bf16[1040,128]{1,0:T(8,128)(2,1)S(1)} %get-tuple-element.1045.refs_4_), channel_id=1, source_target_pairs={{0,112},{4,116},{8,120},{12,124},{16,0},{20,4},{24,8},{28,12},{32,... | collective-permute-start | bytes 798728 | tf_op jit(solution)/shard_map/ppermute | solution.py:142
  21.5 9.8 %collective-permute-start.8 = (bf16[1040,128]{1,0:T(8,128)(2,1)S(1)}, bf16[1040,128]{1,0:T(8,128)(2,1)S(1)}, u32[]{:S(2)}, u32[]{:S(2)}) collective-permute-start(bf16[1040,128]{1,0:T(8,128)(2,1)S(1)} %collective-permute-done.7.refs_5_), channel_id=1, source_target_pairs={{0,16},{4,20},{8,24},{12,28},{16,32},{20,36},{24,40},{28,44},{32,4... | collective-permute-start | bytes 798728 | tf_op jit(solution)/shard_map/ppermute | solution.py:142
  25.2 10.4 %collective-permute-start.17 = (bf16[1024,128]{1,0:T(8,128)(2,1)S(1)}, bf16[1024,128]{1,0:T(8,128)(2,1)S(1)}, u32[]{:S(2)}, u32[]{:S(2)}) collective-permute-start(bf16[1024,128]{1,0:T(8,128)(2,1)S(1)} %get-tuple-element.1048.refs_0_), channel_id=1, source_target_pairs={{0,112},{4,116},{8,120},{12,124},{16,0},{20,4},{24,8},{28,12},{32,... | collective-permute-start | bytes 786440 | tf_op jit(solution)/shard_map/ppermute | solution.py:142
  25.5 15.8 %collective-permute-start.12 = (bf16[1040,128]{1,0:T(8,128)(2,1)S(1)}, bf16[1040,128]{1,0:T(8,128)(2,1)S(1)}, u32[]{:S(2)}, u32[]{:S(2)}) collective-permute-start(bf16[1040,128]{1,0:T(8,128)(2,1)S(1)} %collective-permute-done.11.refs_11_), channel_id=1, source_target_pairs={{0,112},{4,116},{8,120},{12,124},{16,0},{20,4},{24,8},{28,12},{32,... | collective-permute-start | bytes 798728 | tf_op jit(solution)/shard_map/ppermute | solution.py:142
  31.3 10.5 %collective-permute-start.9 = (bf16[1040,128]{1,0:T(8,128)(2,1)S(1)}, bf16[1040,128]{1,0:T(8,128)(2,1)S(1)}, u32[]{:S(2)}, u32[]{:S(2)}) collective-permute-start(bf16[1040,128]{1,0:T(8,128)(2,1)S(1)} %collective-permute-done.8.refs_6_), channel_id=1, source_target_pairs={{0,16},{4,20},{8,24},{12,28},{16,32},{20,36},{24,40},{28,44},{32,4... | collective-permute-start | bytes 798728 | tf_op jit(solution)/shard_map/ppermute | solution.py:142
  35.0 12.4 %collective-permute-start.14 = (bf16[1024,128]{1,0:T(8,128)(2,1)S(1)}, bf16[1024,128]{1,0:T(8,128)(2,1)S(1)}, u32[]{:S(2)}, u32[]{:S(2)}) collective-permute-start(bf16[1024,128]{1,0:T(8,128)(2,1)S(1)} %get-tuple-element.1048.refs_0_), channel_id=1, source_target_pairs={{0,16},{4,20},{8,24},{12,28},{16,32},{20,36},{24,40},{28,44},{32,4... | collective-permute-start | bytes 786440 | tf_op jit(solution)/shard_map/ppermute | solution.py:142
  35.6 15.5 %collective-permute-start.18 = (bf16[1024,128]{1,0:T(8,128)(2,1)S(1)}, bf16[1024,128]{1,0:T(8,128)(2,1)S(1)}, u32[]{:S(2)}, u32[]{:S(2)}) collective-permute-start(bf16[1024,128]{1,0:T(8,128)(2,1)S(1)} %collective-permute-done.17.refs_7_), channel_id=1, source_target_pairs={{0,112},{4,116},{8,120},{12,124},{16,0},{20,4},{24,8},{28,12},{32,... | collective-permute-start | bytes 786440 | tf_op jit(solution)/shard_map/ppermute | solution.py:142
  41.3 23.3 %collective-permute-start.13 = (bf16[1040,128]{1,0:T(8,128)(2,1)S(1)}, bf16[1040,128]{1,0:T(8,128)(2,1)S(1)}, u32[]{:S(2)}, u32[]{:S(2)}) collective-permute-start(bf16[1040,128]{1,0:T(8,128)(2,1)S(1)} %collective-permute-done.12.refs_10_), channel_id=1, source_target_pairs={{0,112},{4,116},{8,120},{12,124},{16,0},{20,4},{24,8},{28,12},{32,... | collective-permute-start | bytes 798728 | tf_op jit(solution)/shard_map/ppermute | solution.py:142
  41.8 22.9 %collective-permute-start.10 = (bf16[1040,128]{1,0:T(8,128)(2,1)S(1)}, bf16[1040,128]{1,0:T(8,128)(2,1)S(1)}, u32[]{:S(2)}, u32[]{:S(2)}) collective-permute-start(bf16[1040,128]{1,0:T(8,128)(2,1)S(1)} %collective-permute-done.9.refs_7_), channel_id=1, source_target_pairs={{0,16},{4,20},{8,24},{12,28},{16,32},{20,36},{24,40},{28,44},{32,4... | collective-permute-start | bytes 798728 | tf_op jit(solution)/shard_map/ppermute | solution.py:147
  47.4 22.1 %collective-permute-start.15 = (bf16[1024,128]{1,0:T(8,128)(2,1)S(1)}, bf16[1024,128]{1,0:T(8,128)(2,1)S(1)}, u32[]{:S(2)}, u32[]{:S(2)}) collective-permute-start(bf16[1024,128]{1,0:T(8,128)(2,1)S(1)} %collective-permute-done.14.refs_1_), channel_id=1, source_target_pairs={{0,16},{4,20},{8,24},{12,28},{16,32},{20,36},{24,40},{28,44},{32,4... | collective-permute-start | bytes 786440 | tf_op jit(solution)/shard_map/ppermute | solution.py:142
  51.1 21.6 %collective-permute-start.19 = (bf16[1024,128]{1,0:T(8,128)(2,1)S(1)}, bf16[1024,128]{1,0:T(8,128)(2,1)S(1)}, u32[]{:S(2)}, u32[]{:S(2)}) collective-permute-start(bf16[1024,128]{1,0:T(8,128)(2,1)S(1)} %collective-permute-done.18.refs_6_), channel_id=1, source_target_pairs={{0,112},{4,116},{8,120},{12,124},{16,0},{20,4},{24,8},{28,12},{32,... | collective-permute-start | bytes 786440 | tf_op jit(solution)/shard_map/ppermute | solution.py:142
  51.1 4.9 %collective-permute-start.4 = (s32[8]{0:T(128)S(1)}, s32[8]{0:T(128)S(1)}, u32[]{:S(2)}, u32[]{:S(2)}) collective-permute-start(s32[8]{0:T(128)S(1)} %get-tuple-element.1044.refs_0_.list_ref), channel_id=1, source_target_pairs={{0,12},{4,0},{8,4},{12,8},{16,28},{20,16},{24,20},{28,24},{32,44},... | collective-permute-start | bytes 104 | tf_op jit(solution)/shard_map/ppermute | solution.py:780
  56.0 5.1 %collective-permute-start.5 = (s32[8]{0:T(128)S(1)}, s32[8]{0:T(128)S(1)}, u32[]{:S(2)}, u32[]{:S(2)}) collective-permute-start(s32[8]{0:T(128)S(1)} %get-tuple-element.1044.refs_0_.list_ref), channel_id=1, source_target_pairs={{0,8},{4,12},{8,0},{12,4},{16,24},{20,28},{24,16},{28,20},{32,40},... | collective-permute-start | bytes 104 | tf_op jit(solution)/shard_map/ppermute | solution.py:780
  67.9 16.1 %collective-permute-start.21 = (bf16[1040,128]{1,0:T(8,128)(2,1)S(1)}, bf16[1040,128]{1,0:T(8,128)(2,1)S(1)}, u32[]{:S(2)}, u32[]{:S(2)}) collective-permute-start(bf16[1040,128]{1,0:T(8,128)(2,1)S(1)} %get-tuple-element.1051), channel_id=1, source_target_pairs={{0,4},{4,8},{8,12},{12,0},{16,20},{20,24},{24,28},{28,16},{32,36},... | collective-permute-start | bytes 798728 | tf_op jit(solution)/shard_map/ppermute | solution.py:790
  69.5 7.1 %collective-permute-start.16 = (bf16[1024,128]{1,0:T(8,128)(2,1)S(1)}, bf16[1024,128]{1,0:T(8,128)(2,1)S(1)}, u32[]{:S(2)}, u32[]{:S(2)}) collective-permute-start(bf16[1024,128]{1,0:T(8,128)(2,1)S(1)} %collective-permute-done.15.refs_2_), channel_id=1, source_target_pairs={{0,16},{4,20},{8,24},{12,28},{16,32},{20,36},{24,40},{28,44},{32,4... | collective-permute-start | bytes 786440 | tf_op jit(solution)/shard_map/ppermute | solution.py:142
  72.7 7.6 %collective-permute-start.20 = (bf16[1024,128]{1,0:T(8,128)(2,1)S(1)}, bf16[1024,128]{1,0:T(8,128)(2,1)S(1)}, u32[]{:S(2)}, u32[]{:S(2)}) collective-permute-start(bf16[1024,128]{1,0:T(8,128)(2,1)S(1)} %collective-permute-done.19.refs_5_), channel_id=1, source_target_pairs={{0,112},{4,116},{8,120},{12,124},{16,0},{20,4},{24,8},{28,12},{32,... | collective-permute-start | bytes 786440 | tf_op jit(solution)/shard_map/ppermute | solution.py:148
  72.7 20.6 %collective-permute-start.22 = (bf16[1040,128]{1,0:T(8,128)(2,1)S(1)}, bf16[1040,128]{1,0:T(8,128)(2,1)S(1)}, u32[]{:S(2)}, u32[]{:S(2)}) collective-permute-start(bf16[1040,128]{1,0:T(8,128)(2,1)S(1)} %get-tuple-element.1052), channel_id=1, source_target_pairs={{0,8},{4,12},{8,0},{12,4},{16,24},{20,28},{24,16},{28,20},{32,40},... | collective-permute-start | bytes 798728 | tf_op jit(solution)/shard_map/ppermute | solution.py:790
  73.6 19.6 %collective-permute-start.23 = (bf16[1040,128]{1,0:T(8,128)(2,1)S(1)}, bf16[1040,128]{1,0:T(8,128)(2,1)S(1)}, u32[]{:S(2)}, u32[]{:S(2)}) collective-permute-start(bf16[1040,128]{1,0:T(8,128)(2,1)S(1)} %get-tuple-element.1053), channel_id=1, source_target_pairs={{0,12},{4,0},{8,4},{12,8},{16,28},{20,16},{24,20},{28,24},{32,44},... | collective-permute-start | bytes 798728 | tf_op jit(solution)/shard_map/ppermute | solution.py:790
  81.3 20.2 %collective-permute-start.24 = (bf16[1024,128]{1,0:T(8,128)(2,1)S(1)}, bf16[1024,128]{1,0:T(8,128)(2,1)S(1)}, u32[]{:S(2)}, u32[]{:S(2)}) collective-permute-start(bf16[1024,128]{1,0:T(8,128)(2,1)S(1)} %get-tuple-element.1056), channel_id=1, source_target_pairs={{0,4},{4,8},{8,12},{12,0},{16,20},{20,24},{24,28},{28,16},{32,36},... | collective-permute-start | bytes 786440 | tf_op jit(solution)/shard_map/ppermute | solution.py:794
  81.4 20.0 %collective-permute-start.25 = (bf16[1024,128]{1,0:T(8,128)(2,1)S(1)}, bf16[1024,128]{1,0:T(8,128)(2,1)S(1)}, u32[]{:S(2)}, u32[]{:S(2)}) collective-permute-start(bf16[1024,128]{1,0:T(8,128)(2,1)S(1)} %get-tuple-element.1057), channel_id=1, source_target_pairs={{0,8},{4,12},{8,0},{12,4},{16,24},{20,28},{24,16},{28,20},{32,40},... | collective-permute-start | bytes 786440 | tf_op jit(solution)/shard_map/ppermute | solution.py:794
  84.0 17.5 %collective-permute-start.26 = (bf16[1024,128]{1,0:T(8,128)(2,1)S(1)}, bf16[1024,128]{1,0:T(8,128)(2,1)S(1)}, u32[]{:S(2)}, u32[]{:S(2)}) collective-permute-start(bf16[1024,128]{1,0:T(8,128)(2,1)S(1)} %get-tuple-element.1058), channel_id=1, source_target_pairs={{0,12},{4,0},{8,4},{12,8},{16,28},{20,16},{24,20},{28,24},{32,44},... | collective-permute-start | bytes 786440 | tf_op jit(solution)/shard_map/ppermute | solution.py:794
  115.5 9.8 %collective-permute-start.33 = (bf16[64,2048]{1,0:T(8,128)(2,1)S(1)}, bf16[64,2048]{1,0:T(8,128)(2,1)S(1)}, u32[]{:S(2)}, u32[]{:S(2)}) collective-permute-start(bf16[64,2048]{1,0:T(8,128)(2,1)S(1)} %get-tuple-element.1076), channel_id=1, source_target_pairs={{0,3},{1,0},{2,1},{3,2},{4,7},{5,4},{6,5},{7,6},{8,11},{9,8},{10,9... | collective-permute-start | bytes 786440 | tf_op jit(solution)/shard_map/ppermute | solution.py:810
  118.6 12.3 %collective-permute-start.32 = (bf16[64,2048]{1,0:T(8,128)(2,1)S(1)}, bf16[64,2048]{1,0:T(8,128)(2,1)S(1)}, u32[]{:S(2)}, u32[]{:S(2)}) collective-permute-start(bf16[64,2048]{1,0:T(8,128)(2,1)S(1)} %get-tuple-element.1075), channel_id=1, source_target_pairs={{0,3},{1,0},{2,1},{3,2},{4,7},{5,4},{6,5},{7,6},{8,11},{9,8},{10,9... | collective-permute-start | bytes 786440 | tf_op jit(solution)/shard_map/ppermute | solution.py:807
  119.3 15.5 %collective-permute-start.30 = (bf16[64,2048]{1,0:T(8,128)(2,1)S(1)}, bf16[64,2048]{1,0:T(8,128)(2,1)S(1)}, u32[]{:S(2)}, u32[]{:S(2)}) collective-permute-start(bf16[64,2048]{1,0:T(8,128)(2,1)S(1)} %get-tuple-element.1073), channel_id=1, source_target_pairs={{0,1},{1,2},{2,3},{3,0},{4,5},{5,6},{6,7},{7,4},{8,9},{9,10},{10,1... | collective-permute-start | bytes 786440 | tf_op jit(solution)/shard_map/ppermute | solution.py:809
  120.6 14.7 %collective-permute-start.29 = (bf16[64,2048]{1,0:T(8,128)(2,1)S(1)}, bf16[64,2048]{1,0:T(8,128)(2,1)S(1)}, u32[]{:S(2)}, u32[]{:S(2)}) collective-permute-start(bf16[64,2048]{1,0:T(8,128)(2,1)S(1)} %get-tuple-element.1072), channel_id=1, source_target_pairs={{0,1},{1,2},{2,3},{3,0},{4,5},{5,6},{6,7},{7,4},{8,9},{9,10},{10,1... | collective-permute-start | bytes 786440 | tf_op jit(solution)/shard_map/ppermute | solution.py:806
  120.6 18.5 %collective-permute-start.27 = (bf16[64,4096]{1,0:T(8,128)(2,1)S(1)}, bf16[64,4096]{1,0:T(8,128)(2,1)S(1)}, u32[]{:S(2)}, u32[]{:S(2)}) collective-permute-start(bf16[64,4096]{1,0:T(8,128)(2,1)S(1)} %get-tuple-element.1069), channel_id=1, source_target_pairs={{0,3},{1,0},{2,1},{3,2},{4,7},{5,4},{6,5},{7,6},{8,11},{9,8},{10,9... | collective-permute-start | bytes 1572872 | tf_op jit(solution)/shard_map/ppermute | solution.py:811
  125.3 17.7 %collective-permute-start.28 = (bf16[64,4096]{1,0:T(8,128)(2,1)S(1)}, bf16[64,4096]{1,0:T(8,128)(2,1)S(1)}, u32[]{:S(2)}, u32[]{:S(2)}) collective-permute-start(bf16[64,4096]{1,0:T(8,128)(2,1)S(1)} %get-tuple-element.1070), channel_id=1, source_target_pairs={{0,1},{1,2},{2,3},{3,0},{4,5},{5,6},{6,7},{7,4},{8,9},{9,10},{10,1... | collective-permute-start | bytes 1572872 | tf_op jit(solution)/shard_map/ppermute | solution.py:812
  131.0 13.7 %collective-permute-start.34 = (bf16[64,4096]{1,0:T(8,128)(2,1)S(1)}, bf16[64,4096]{1,0:T(8,128)(2,1)S(1)}, u32[]{:S(2)}, u32[]{:S(2)}) collective-permute-start(bf16[64,4096]{1,0:T(8,128)(2,1)S(1)} %combine.3), channel_id=1, source_target_pairs={{0,3},{1,0},{2,1},{3,2},{4,7},{5,4},{6,5},{7,6},{8,11},{9,8},{10,9... | collective-permute-start | bytes 1572872 | tf_op jit(solution)/shard_map/ppermute | solution.py:814
  135.4 13.2 %collective-permute-start.31 = (bf16[64,4096]{1,0:T(8,128)(2,1)S(1)}, bf16[64,4096]{1,0:T(8,128)(2,1)S(1)}, u32[]{:S(2)}, u32[]{:S(2)}) collective-permute-start(bf16[64,4096]{1,0:T(8,128)(2,1)S(1)} %combine.2), channel_id=1, source_target_pairs={{0,1},{1,2},{2,3},{3,0},{4,5},{5,6},{6,7},{7,4},{8,9},{9,10},{10,1... | collective-permute-start | bytes 1572872 | tf_op jit(solution)/shard_map/ppermute | solution.py:813
  (6 other events, 168.0 us)

commit v2 on v1

--- a/solution.py
+++ b/solution.py
@@ -262,13 +262,10 @@
     )(picks, *srcs)
 
 
-def attend_node(n, tokens, scale, tp, q_ref, nk_ref, nv_ref, kbuf, vbuf, att_ref):
+def attend_nodes(nodes, blocks, tokens, scale, tp, q_ref, nk_ref, nv_ref, kbuf, vbuf, att_ref):
     heads, _, dim = kbuf.shape[1:]
     group = q_ref.shape[1] // (heads * dim)
     per = NODE // NTP
-    at = pl.multiple_of(n * STEP, STEP)
-    to = ((n // per - tp + NTP) % NTP) * per + n % per
-    to = pl.multiple_of(to * STEP, STEP)
     rows = STEP * group
     f32 = jnp.float32
     nt = (((1,), (1,)), ((), ()))
@@ -277,21 +274,26 @@
     step_ok = lax.broadcasted_iota(jnp.int32, (rows, BLK), 1) <= step_of
     pad = jnp.zeros((BLK - STEP, dim), kbuf.dtype)
     rate = scale * math.log2(math.e)
+    chains = [(i, h) for i in range(len(nodes)) for h in range(heads)]
+    at = [pl.multiple_of(n * STEP, STEP) for n in nodes]
     logits = []
-    for h in range(heads):
+    for i, h in chains:
         base = h * group * dim
+        step = pl.ds(at[i], STEP)
         q = jnp.concatenate(
-            [q_ref[pl.ds(at, STEP), base + g * dim : base + (g + 1) * dim] for g in range(group)],
-            axis=0,
+            [q_ref[step, base + g * dim : base + (g + 1) * dim] for g in range(group)], axis=0
         )
-        nk = nk_ref[pl.ds(at, STEP), h * dim : (h + 1) * dim]
-        k = jnp.concatenate([kbuf[n, h, :tokens], nk, pad], axis=0)
+        nk = nk_ref[step, h * dim : (h + 1) * dim]
+        k = jnp.concatenate([kbuf[nodes[i], h, :tokens], nk, pad], axis=0)
         logits.append(lax.dot_general(q, k, nt, preferred_element_type=f32))
     weights = []
     totals = []
-    for h in range(heads):
-        tiles = [logits[h][:, i : i + BLK] for i in range(0, tokens, BLK)]
-        tiles.append(jnp.where(step_ok, logits[h][:, tokens:], -jnp.inf))
+    for (i, h), logit in zip(chains, logits):
+        tiles = [logit[:, :BLK]]
+        for b in range(1, tokens // BLK):
+            tile = logit[:, b * BLK : (b + 1) * BLK]
+            tiles.append(tile if blocks is None else jnp.where(blocks[i] > b, tile, -jnp.inf))
+        tiles.append(jnp.where(step_ok, logit[:, tokens:], -jnp.inf))
         top = tiles[0]
         for tile in tiles[1:]:
             top = jnp.maximum(top, tile)
@@ -302,16 +304,44 @@
             total = total + tile
         totals.append(jnp.sum(total, axis=1, keepdims=True))
         weights.append(jnp.concatenate([tile.astype(kbuf.dtype) for tile in tiles], axis=1))
-    for h in range(heads):
+    for c, (i, h) in enumerate(chains):
         base = h * group * dim
-        nv = nv_ref[pl.ds(at, STEP), h * dim : (h + 1) * dim]
-        v = jnp.concatenate([vbuf[n, h, :tokens], nv, pad], axis=0)
-        o = lax.dot_general(weights[h], v, nn, preferred_element_type=f32)
-        o = (o * (1.0 / totals[h])).astype(att_ref.dtype)
+        nv = nv_ref[pl.ds(at[i], STEP), h * dim : (h + 1) * dim]
+        v = jnp.concatenate([vbuf[nodes[i], h, :tokens], nv, pad], axis=0)
+        o = lax.dot_general(weights[c], v, nn, preferred_element_type=f32)
+        o = (o * (1.0 / totals[c])).astype(att_ref.dtype)
+        to = ((nodes[i] // per - tp + NTP) % NTP) * per + nodes[i] % per
+        to = pl.ds(pl.multiple_of(to * STEP, STEP), STEP)
         for g in range(group):
-            att_ref[pl.ds(to, STEP), base + g * dim : base + (g + 1) * dim] = o[
-                g * STEP : (g + 1) * STEP
-            ]
+            att_ref[to, base + g * dim : base + (g + 1) * dim] = o[g * STEP : (g + 1) * STEP]
+
+
+def attend_pairs(chosen, wait, todo_ref, run):
+    def collect(n, count):
+        take = chosen(n)
+
+        @pl.when(take)
+        def _():
+            todo_ref[count] = n
+            todo_ref[count + 1] = n
+
+        return count + take.astype(jnp.int32)
+
+    count = lax.fori_loop(0, NODE, collect, jnp.int32(0))
+
+    def pair(p, carry):
+        one = todo_ref[2 * p]
+        two = todo_ref[2 * p + 1]
+        wait(one)
+
+        @pl.when(two != one)
+        def _():
+            wait(two)
+
+        run((one, two))
+        return carry
+
+    lax.fori_loop(0, (count + 1) // 2, pair, 0)
 
 
 def cache_copies(src, j, bufs, sems):
@@ -351,7 +381,8 @@
 def local_body(scale, where_ref, list_ref, blocks_ref, q_ref, nk_ref, nv_ref, *refs):
     caches = refs[0:2]
     moved = refs[2:4]
-    w_ref, att_ref, w0_ref, table_ref, kbuf, vbuf, wide_ref, ids_ref, sems, sem, wsem = refs[4:]
+    w_ref, att_ref, w0_ref, table_ref = refs[4:8]
+    kbuf, vbuf, wide_ref, ids_ref, todo_ref, sems, sem, wsem = refs[8:]
     bufs = (kbuf, vbuf)
     here = where_ref[1]
     tp = where_ref[2]
@@ -391,35 +422,35 @@
     for i in range(T_FIT, T_SIZE):
         table_ref[i] = ids_ref[0, FAST]
 
-    def node(n):
-        dist = table_ref[T_FROM + n]
-        blocks = jnp.where(dist == NX, blocks_ref[n], ids_ref[0, table_ref[T_RANK + n]])
+    def measure(n):
+        blocks = jnp.where(
+            table_ref[T_FROM + n] == NX, blocks_ref[n], ids_ref[0, table_ref[T_RANK + n]]
+        )
         table_ref[T_LEN + n] = blocks
-        mine = (dist == NX) | (dist == 0)
-        run = functools.partial(
-            attend_node, n, scale=scale, tp=tp, q_ref=q_ref, nk_ref=nk_ref, nv_ref=nv_ref,
-            kbuf=kbuf, vbuf=vbuf, att_ref=att_ref,
-        )
-
-        @pl.when(dist == NX)
+
+    each_node(measure)
+
+    def chosen(n):
+        return (table_ref[T_FROM + n] == NX) | (table_ref[T_FROM + n] == 0)
+
+    def wait(n):
+        @pl.when(table_ref[T_FROM + n] == NX)
         def _():
             for c in cache_copies(caches, n, bufs, sems):
                 c.wait()
 
-        @pl.when(dist == 0)
+        @pl.when(table_ref[T_FROM + n] == 0)
         def _():
             for c in moved_copies(moved, 0, n, bufs, sems):
                 c.wait()
 
-        @pl.when(mine & (blocks == 2))
-        def _():
-            run(tokens=2 * BLK)
-
-        @pl.when(mine & (blocks == 1))
-        def _():
-            run(tokens=BLK)
-
-    each_node(node)
+    def run(nodes):
+        blocks = [table_ref[T_LEN + n] for n in nodes]
+        attend_nodes(
+            nodes, blocks, 2 * BLK, scale, tp, q_ref, nk_ref, nv_ref, kbuf, vbuf, att_ref
+        )
+
+    attend_pairs(chosen, wait, todo_ref, run)
     load.wait()
 
 
@@ -433,6 +464,7 @@
         pltpu.VMEM(keys.shape, keys.dtype),
         pltpu.VMEM((NX, 128), jnp.int32),
         pltpu.SMEM((NX, 128), jnp.int32),
+        pltpu.SMEM((NODE + 2,), jnp.int32),
         pltpu.SemaphoreType.DMA((NODE, per_node)),
         pltpu.SemaphoreType.DMA,
         pltpu.SemaphoreType.DMA,
@@ -458,7 +490,8 @@
 def early_body(scale, where_ref, old_table, q_ref, nk_ref, nv_ref, *refs):
     moved = refs[: NX - 1]
     refs = refs[NX - 1 :]
-    w_ref, old_ref, att_ref, w1_ref, table_ref, kbuf, vbuf, wide_ref, ids_ref, sems, sem, wsem = refs
+    w_ref, old_ref, att_ref, w1_ref, table_ref = refs[:5]
+    kbuf, vbuf, wide_ref, ids_ref, todo_ref, sems, sem, wsem = refs[5:]
     del old_ref
     bufs = (kbuf, vbuf)
 
@@ -483,25 +516,35 @@
     for i in range(T_FIT, T_SIZE):
         table_ref[i] = fit
 
-    def node(n):
-        dist = old_table[T_FROM + n]
-        far = (dist > 0) & (dist < NX)
-        at = jnp.clip(dist - 1, 0, NX - 2)
-        blocks = jnp.where(far, ids_ref[at, old_table[T_RANK + n]], old_table[T_LEN + n])
+    def is_far(n):
+        return (old_table[T_FROM + n] > 0) & (old_table[T_FROM + n] < NX)
+
+    def wait(n):
+        for c in moved_copies(moved[:1], 0, n, bufs, sems):
+            c.wait()
+
+    def measure(n):
+        at = jnp.clip(old_table[T_FROM + n] - 1, 0, NX - 2)
+        blocks = jnp.where(
+            is_far(n), ids_ref[at, old_table[T_RANK + n]], old_table[T_LEN + n]
+        )
         table_ref[T_LEN + n] = blocks
 
-        @pl.when(far)
+        @pl.when(is_far(n) & (blocks == 2))
         def _():
-            for c in moved_copies(moved[:1], 0, n, bufs, sems):
-                c.wait()
-
-        @pl.when(far & (blocks == 1))
-        def _():
-            attend_node(
-                n, BLK, scale, where_ref[2], q_ref, nk_ref, nv_ref, kbuf, vbuf, att_ref
-            )
-
-    each_node(node)
+            wait(n)
+
+    each_node(measure)
+
+    def chosen(n):
+        return is_far(n) & (table_ref[T_LEN + n] == 1)
+
+    def run(nodes):
+        attend_nodes(
+            nodes, None, BLK, scale, where_ref[2], q_ref, nk_ref, nv_ref, kbuf, vbuf, att_ref
+        )
+
+    attend_pairs(chosen, wait, todo_ref, run)
     load.wait()
 
 
@@ -548,7 +591,7 @@
     seconds = refs[far : 2 * far]
     old_ref, w_ref, att_ref = refs[2 * far : 2 * far + 3]
     outs = refs[2 * far + 3 : 2 * far + 10]
-    kbuf, vbuf, sems = refs[2 * far + 10 :]
+    kbuf, vbuf, todo_ref, sems = refs[2 * far + 10 :]
     del old_ref
     bufs = (kbuf, vbuf)
 
@@ -567,16 +610,16 @@
 
     each_node(start)
 
-    def node(n):
-        @pl.when(is_late(n))
-        def _():
-            for c in moved_copies((firsts[0], seconds[0]), 0, n, bufs, sems):
-                c.wait()
-            attend_node(
-                n, 2 * BLK, scale, where_ref[2], q_ref, nk_ref, nv_ref, kbuf, vbuf, att_ref
-            )
-
-    each_node(node)
+    def wait(n):
+        for c in moved_copies((firsts[0], seconds[0]), 0, n, bufs, sems):
+            c.wait()
+
+    def run(nodes):
+        attend_nodes(
+            nodes, None, 2 * BLK, scale, where_ref[2], q_ref, nk_ref, nv_ref, kbuf, vbuf, att_ref
+        )
+
+    attend_pairs(is_late, wait, todo_ref, run)
     project_half(0, tile, att_ref, w_ref, *outs)
 
 
@@ -595,6 +638,7 @@
         scratch_shapes=[
             pltpu.VMEM(shape, dtype),
             pltpu.VMEM(shape, dtype),
+            pltpu.SMEM((NODE + 2,), jnp.int32),
             pltpu.SemaphoreType.DMA((NODE, 4 * shape[1])),
         ],
         input_output_aliases={5 + 2 * far: 0},

time: 153 us -> 152 us (level)
  no operation moved by 1% of the time
where the time goes in v2:
time: 152 us; the launch traced here: 150 us
  waiting for transfers between devices  63.7 us (42%)
  starting transfers between devices  44.4 us (29%)
  Pallas kernels  39.8 us (26%)
    ppermute x6, waiting for transfers between devices, ring_step(): lax.ppermute(up, 'slot', zperm(1))  17.1 us
    ppermute x6, starting transfers between devices, ring_step(): lax.ppermute(up, 'slot', zperm(1))  16 us
    ppermute x3, waiting for transfers between devices, shards(): lists.append(lax.ppermute(own_list, 'slot', xperm(-d)))  11.1 us
    pallas_call x1, Pallas kernels, local(): pl.pallas_call(functools.partial(local_body, float(keys.shape[3]) ** (-0....  9.23 us
    pallas_call x1, Pallas kernels, late(): pl.pallas_call(functools.partial(late_body, float(shape[3]) ** (-0.5), ti...  8.4 us
    ppermute x1, waiting for transfers between devices, shards(): mine = lax.ppermute(fork_src, ('role', 'slot'), halves_perm(0, n_slot))  8.29 us
    pallas_call x1, Pallas kernels, early(): pl.pallas_call(functools.partial(early_body, float(keys.shape[3]) ** (-0....  8.15 us
    pallas_call x1, Pallas kernels, project(): pl.pallas_call(functools.partial(project_body, tile), out_shape=(wide, sl...  5.77 us
  transfers between devices with their start and end apart: 33, of which 20 were waited for; matrix products, arithmetic and copies ran while one was open for 0% of the time, Pallas kernels for 15%

profile of v2, /device:TPU:102, one launch (start us, length us, event | category | flops | bytes accessed | tf_op | source)
XLA Modules:
  0.0 150.1 jit_solution(4715773584130841837)
XLA Ops:
  0.7 1.9 %collective-permute-start.2 = (s32[4]{0:T(128)}, s32[4]{0:T(128)S(1)}, u32[]{:S(2)}, u32[]{:S(2)}) collective-permute-start(s32[4]{0:T(128)} %param.28), channel_id=1, source_target_pairs={{0,0},{4,128},{8,4},{12,132},{16,8},{20,136},{24,12},{28,140},{32,... | collective-permute-start | bytes 56 | tf_op jit(solution)/shard_map/ppermute | solution.py:817
  2.8 8.3 %collective-permute-done.2.mine_ref = s32[4]{0:T(128)S(1)} collective-permute-done((s32[4]{0:T(128)}, s32[4]{0:T(128)S(1)}, u32[]{:S(2)}, u32[]{:S(2)}) %collective-permute-start.2) | collective-permute-done | bytes 48 | tf_op jit(solution)/shard_map/ppermute | solution.py:817
  11.1 2.4 %pack.3 = (bf16[1040,128]{1,0:T(8,128)(2,1)S(1)}, bf16[1024,128]{1,0:T(8,128)(2,1)S(1)}, s32[8]{0:T(128)S(1)}) custom-call(s32[3]{0:T(128)S(1)} %pad_add_fusion.where_ref, s32[4]{0:T(128)S(1)} %collective-permute-done.2.mine_ref, s32[4]{0:T(128)S(1)} %collective-permute-done.3.other_ref, s32[8]{0:T(128)S(1)} %copy.83.blocks_ref, ...), custom_call_target="tpu_custom_call" | custom-call | tf_op jit(solution)/shard_map/pack/pallas_call | solution.py:125
  13.4 1.7 %collective-permute-start.7 = (bf16[1040,128]{1,0:T(8,128)(2,1)S(1)}, bf16[1040,128]{1,0:T(8,128)(2,1)S(1)}, u32[]{:S(2)}, u32[]{:S(2)}) collective-permute-start(bf16[1040,128]{1,0:T(8,128)(2,1)S(1)} %get-tuple-element.1045.refs_4_), channel_id=1, source_target_pairs={{0,16},{4,20},{8,24},{12,28},{16,32},{20,36},{24,40},{28,44},{32,4... | collective-permute-start | bytes 798728 | tf_op jit(solution)/shard_map/ppermute | solution.py:142
  15.5 6.0 %collective-permute-done.7.refs_5_ = bf16[1040,128]{1,0:T(8,128)(2,1)S(1)} collective-permute-done((bf16[1040,128]{1,0:T(8,128)(2,1)S(1)}, bf16[1040,128]{1,0:T(8,128)(2,1)S(1)}, u32[]{:S(2)}, u32[]{:S(2)}) %collective-permute-start.7) | collective-permute-done | bytes 266272 | tf_op jit(solution)/shard_map/ppermute | solution.py:142
  21.5 3.7 %collective-permute-start.8 = (bf16[1040,128]{1,0:T(8,128)(2,1)S(1)}, bf16[1040,128]{1,0:T(8,128)(2,1)S(1)}, u32[]{:S(2)}, u32[]{:S(2)}) collective-permute-start(bf16[1040,128]{1,0:T(8,128)(2,1)S(1)} %collective-permute-done.7.refs_5_), channel_id=1, source_target_pairs={{0,16},{4,20},{8,24},{12,28},{16,32},{20,36},{24,40},{28,44},{32,4... | collective-permute-start | bytes 798728 | tf_op jit(solution)/shard_map/ppermute | solution.py:142
  25.5 5.8 %collective-permute-done.8.refs_6_ = bf16[1040,128]{1,0:T(8,128)(2,1)S(1)} collective-permute-done((bf16[1040,128]{1,0:T(8,128)(2,1)S(1)}, bf16[1040,128]{1,0:T(8,128)(2,1)S(1)}, u32[]{:S(2)}, u32[]{:S(2)}) %collective-permute-start.8) | collective-permute-done | bytes 266272 | tf_op jit(solution)/shard_map/ppermute | solution.py:142
  31.3 3.7 %collective-permute-start.9 = (bf16[1040,128]{1,0:T(8,128)(2,1)S(1)}, bf16[1040,128]{1,0:T(8,128)(2,1)S(1)}, u32[]{:S(2)}, u32[]{:S(2)}) collective-permute-start(bf16[1040,128]{1,0:T(8,128)(2,1)S(1)} %collective-permute-done.8.refs_6_), channel_id=1, source_target_pairs={{0,16},{4,20},{8,24},{12,28},{16,32},{20,36},{24,40},{28,44},{32,4... | collective-permute-start | bytes 798728 | tf_op jit(solution)/shard_map/ppermute | solution.py:142
  37.0 4.3 %collective-permute-done.12.refs_10_ = bf16[1040,128]{1,0:T(8,128)(2,1)S(1)} collective-permute-done((bf16[1040,128]{1,0:T(8,128)(2,1)S(1)}, bf16[1040,128]{1,0:T(8,128)(2,1)S(1)}, u32[]{:S(2)}, u32[]{:S(2)}) %collective-permute-start.12) | collective-permute-done | bytes 266272 | tf_op jit(solution)/shard_map/ppermute | solution.py:142
  41.8 3.7 %collective-permute-start.10 = (bf16[1040,128]{1,0:T(8,128)(2,1)S(1)}, bf16[1040,128]{1,0:T(8,128)(2,1)S(1)}, u32[]{:S(2)}, u32[]{:S(2)}) collective-permute-start(bf16[1040,128]{1,0:T(8,128)(2,1)S(1)} %collective-permute-done.9.refs_7_), channel_id=1, source_target_pairs={{0,16},{4,20},{8,24},{12,28},{16,32},{20,36},{24,40},{28,44},{32,4... | collective-permute-start | bytes 798728 | tf_op jit(solution)/shard_map/ppermute | solution.py:147
  45.5 1.9 %collective-permute-done.14.refs_1_ = bf16[1024,128]{1,0:T(8,128)(2,1)S(1)} collective-permute-done((bf16[1024,128]{1,0:T(8,128)(2,1)S(1)}, bf16[1024,128]{1,0:T(8,128)(2,1)S(1)}, u32[]{:S(2)}, u32[]{:S(2)}) %collective-permute-start.14) | collective-permute-done | bytes 262176 | tf_op jit(solution)/shard_map/ppermute | solution.py:142
  47.4 3.7 %collective-permute-start.15 = (bf16[1024,128]{1,0:T(8,128)(2,1)S(1)}, bf16[1024,128]{1,0:T(8,128)(2,1)S(1)}, u32[]{:S(2)}, u32[]{:S(2)}) collective-permute-start(bf16[1024,128]{1,0:T(8,128)(2,1)S(1)} %collective-permute-done.14.refs_1_), channel_id=1, source_target_pairs={{0,16},{4,20},{8,24},{12,28},{16,32},{20,36},{24,40},{28,44},{32,4... | collective-permute-start | bytes 786440 | tf_op jit(solution)/shard_map/ppermute | solution.py:142
  52.8 3.2 %collective-permute-done.4.refs_1_ = s32[8]{0:T(128)S(1)} collective-permute-done((s32[8]{0:T(128)S(1)}, s32[8]{0:T(128)S(1)}, u32[]{:S(2)}, u32[]{:S(2)}) %collective-permute-start.4) | collective-permute-done | bytes 64 | tf_op jit(solution)/shard_map/ppermute | solution.py:824
  56.4 4.7 %collective-permute-done.5.refs_2_ = s32[8]{0:T(128)S(1)} collective-permute-done((s32[8]{0:T(128)S(1)}, s32[8]{0:T(128)S(1)}, u32[]{:S(2)}, u32[]{:S(2)}) %collective-permute-start.5) | collective-permute-done | bytes 64 | tf_op jit(solution)/shard_map/ppermute | solution.py:824
  61.3 3.3 %collective-permute-done.6.refs_3_ = s32[8]{0:T(128)S(1)} collective-permute-done((s32[8]{0:T(128)S(1)}, s32[8]{0:T(128)S(1)}, u32[]{:S(2)}, u32[]{:S(2)}) %collective-permute-start.6) | collective-permute-done | bytes 64 | tf_op jit(solution)/shard_map/ppermute | solution.py:824
  64.6 3.2 %select_first.1 = (bf16[1040,128]{1,0:T(8,128)(2,1)S(1)}, bf16[1040,128]{1,0:T(8,128)(2,1)S(1)}, bf16[1040,128]{1,0:T(8,128)(2,1)S(1)}, bf16[1040,128]{1,0:T(8,128)(2,1)S(1)}, s32[16]{0:T(128)S(1)}) custom-call(s32[3]{0:T(128)S(1)} %pad_add_fusion.where_ref, s32[8]{0:T(128)S(1)} %get-tuple-element.1044.refs_0_.list_ref, ...), custom_call_target="tpu_custom_call" | custom-call | tf_op jit(solution)/shard_map/select_first/pallas_call | solution.py:233
  69.5 3.2 %collective-permute-start.16 = (bf16[1024,128]{1,0:T(8,128)(2,1)S(1)}, bf16[1024,128]{1,0:T(8,128)(2,1)S(1)}, u32[]{:S(2)}, u32[]{:S(2)}) collective-permute-start(bf16[1024,128]{1,0:T(8,128)(2,1)S(1)} %collective-permute-done.15.refs_2_), channel_id=1, source_target_pairs={{0,16},{4,20},{8,24},{12,28},{16,32},{20,36},{24,40},{28,44},{32,4... | collective-permute-start | bytes 786440 | tf_op jit(solution)/shard_map/ppermute | solution.py:142
  73.6 2.9 %collective-permute-done.16.refs_3_ = bf16[1024,128]{1,0:T(8,128)(2,1)S(1)} collective-permute-done((bf16[1024,128]{1,0:T(8,128)(2,1)S(1)}, bf16[1024,128]{1,0:T(8,128)(2,1)S(1)}, u32[]{:S(2)}, u32[]{:S(2)}) %collective-permute-start.16) | collective-permute-done | bytes 262176 | tf_op jit(solution)/shard_map/ppermute | solution.py:142
  76.6 3.7 %collective-permute-done.20.refs_4_ = bf16[1024,128]{1,0:T(8,128)(2,1)S(1)} collective-permute-done((bf16[1024,128]{1,0:T(8,128)(2,1)S(1)}, bf16[1024,128]{1,0:T(8,128)(2,1)S(1)}, u32[]{:S(2)}, u32[]{:S(2)}) %collective-permute-start.20) | collective-permute-done | bytes 262176 | tf_op jit(solution)/shard_map/ppermute | solution.py:148
  81.4 2.5 %collective-permute-start.25 = (bf16[1024,128]{1,0:T(8,128)(2,1)S(1)}, bf16[1024,128]{1,0:T(8,128)(2,1)S(1)}, u32[]{:S(2)}, u32[]{:S(2)}) collective-permute-start(bf16[1024,128]{1,0:T(8,128)(2,1)S(1)} %get-tuple-element.1057), channel_id=1, source_target_pairs={{0,8},{4,12},{8,0},{12,4},{16,24},{20,28},{24,16},{28,20},{32,40},... | collective-permute-start | bytes 786440 | tf_op jit(solution)/shard_map/ppermute | solution.py:838
  84.0 9.2 %local.1 = (bf16[256,2048]{1,0:T(8,128)(2,1)S(1)}, bf16[2048,4096]{1,0:T(8,128)(2,1)S(1)}, s32[32]{0:T(128)S(1)}) custom-call(s32[3]{0:T(128)S(1)} %pad_add_fusion.where_ref, s32[8]{0:T(128)S(1)} %get-tuple-element.1044.refs_0_.list_ref, s32[8]{0:T(128)S(1)} %copy.83.blocks_ref, bf16[256,2048]{1,0:T(8,128)(2,1)S(1)} %bitcast.71, ...), custom_call_target="tpu_custom_call" | custom-call | tf_op jit(solution)/shard_map/local/pallas_call | solution.py:475
  93.3 8.2 %early.1 = (bf16[256,2048]{1,0:T(8,128)(2,1)S(1)}, bf16[2048,4096]{1,0:T(8,128)(2,1)S(1)}, s32[32]{0:T(128)S(1)}) custom-call(s32[3]{0:T(128)S(1)} %pad_add_fusion.where_ref, s32[32]{0:T(128)S(1)} %get-tuple-element.1050.old_table, bf16[256,2048]{1,0:T(8,128)(2,1)S(1)} %bitcast.72, bf16[256,256]{1,0:T(8,128)(2,1)S(1)} %bitcast.79, ...), custom_call_target="tpu_custom_call", output_to_operand_aliasing={{0}: (9, {})} | custom-call | tf_op jit(solution)/shard_map/early/pallas_call | solution.py:552
  101.5 8.4 %late.1 = (bf16[256,2048]{1,0:T(8,128)(2,1)S(1)}, bf16[64,4096]{1,0:T(8,128)(2,1)S(1)}, bf16[64,2048]{1,0:T(8,128)(2,1)S(1)}, bf16[64,2048]{1,0:T(8,128)(2,1)S(1...) custom-call(s32[3]{0:T(128)S(1)} %pad_add_fusion.where_ref, ...), custom_call_target="tpu_custom_call", output_to_operand_aliasing={{0}: (11, {})} | custom-call | tf_op jit(solution)/shard_map/late/pallas_call | solution.py:633
  109.9 5.8 %project.1 = (bf16[64,4096]{1,0:T(8,128)(2,1)S(1)}, bf16[64,2048]{1,0:T(8,128)(2,1)S(1)}, bf16[64,2048]{1,0:T(8,128)(2,1)S(1)}, bf16[64,4096]{1,0:T(8,128)(2,1)S...) custom-call(bf16[256,2048]{1,0:T(8,128)(2,1)S(1)} %get-tuple-element, ...), custom_call_target="tpu_custom_call", output_to_operand_aliasing={{3}: (2, {}), {4}: (3, {}), {5}: (4, {}), {6}: (5, {})} | custom-call | tf_op jit(solution)/shard_map/project/pallas_call | solution.py:660
  115.6 3.1 %collective-permute-start.33 = (bf16[64,2048]{1,0:T(8,128)(2,1)S(1)}, bf16[64,2048]{1,0:T(8,128)(2,1)S(1)}, u32[]{:S(2)}, u32[]{:S(2)}) collective-permute-start(bf16[64,2048]{1,0:T(8,128)(2,1)S(1)} %get-tuple-element.1076), channel_id=1, source_target_pairs={{0,3},{1,0},{2,1},{3,2},{4,7},{5,4},{6,5},{7,6},{8,11},{9,8},{10,9... | collective-permute-start | bytes 786440 | tf_op jit(solution)/shard_map/ppermute | solution.py:854
  120.8 3.2 %collective-permute-start.27 = (bf16[64,4096]{1,0:T(8,128)(2,1)S(1)}, bf16[64,4096]{1,0:T(8,128)(2,1)S(1)}, u32[]{:S(2)}, u32[]{:S(2)}) collective-permute-start(bf16[64,4096]{1,0:T(8,128)(2,1)S(1)} %get-tuple-element.1069), channel_id=1, source_target_pairs={{0,3},{1,0},{2,1},{3,2},{4,7},{5,4},{6,5},{7,6},{8,11},{9,8},{10,9... | collective-permute-start | bytes 1572872 | tf_op jit(solution)/shard_map/ppermute | solution.py:855
  126.5 4.6 %collective-permute-done.32.low_ref = bf16[64,2048]{1,0:T(8,128)(2,1)S(1)} collective-permute-done((bf16[64,2048]{1,0:T(8,128)(2,1)S(1)}, bf16[64,2048]{1,0:T(8,128)(2,1)S(1)}, u32[]{:S(2)}, u32[]{:S(2)}) %collective-permute-start.32) | collective-permute-done | bytes 262176 | tf_op jit(solution)/shard_map/ppermute | solution.py:851
  131.2 3.8 %collective-permute-start.34 = (bf16[64,4096]{1,0:T(8,128)(2,1)S(1)}, bf16[64,4096]{1,0:T(8,128)(2,1)S(1)}, u32[]{:S(2)}, u32[]{:S(2)}) collective-permute-start(bf16[64,4096]{1,0:T(8,128)(2,1)S(1)} %combine.3), channel_id=1, source_target_pairs={{0,3},{1,0},{2,1},{3,2},{4,7},{5,4},{6,5},{7,6},{8,11},{9,8},{10,9... | collective-permute-start | bytes 1572872 | tf_op jit(solution)/shard_map/ppermute | solution.py:858
  137.0 2.3 %collective-permute-done.27.da = bf16[64,4096]{1,0:T(8,128)(2,1)S(1)} collective-permute-done((bf16[64,4096]{1,0:T(8,128)(2,1)S(1)}, bf16[64,4096]{1,0:T(8,128)(2,1)S(1)}, u32[]{:S(2)}, u32[]{:S(2)}) %collective-permute-start.27) | collective-permute-done | bytes 524320 | tf_op jit(solution)/shard_map/ppermute | solution.py:855
  139.3 3.9 %collective-permute-done.28.db = bf16[64,4096]{1,0:T(8,128)(2,1)S(1)} collective-permute-done((bf16[64,4096]{1,0:T(8,128)(2,1)S(1)}, bf16[64,4096]{1,0:T(8,128)(2,1)S(1)}, u32[]{:S(2)}, u32[]{:S(2)}) %collective-permute-start.28) | collective-permute-done | bytes 524320 | tf_op jit(solution)/shard_map/ppermute | solution.py:856
  143.2 1.7 %collective-permute-done.34.fb = bf16[64,4096]{1,0:T(8,128)(2,1)S(1)} collective-permute-done((bf16[64,4096]{1,0:T(8,128)(2,1)S(1)}, bf16[64,4096]{1,0:T(8,128)(2,1)S(1)}, u32[]{:S(2)}, u32[]{:S(2)}) %collective-permute-start.34) | collective-permute-done | bytes 524320 | tf_op jit(solution)/shard_map/ppermute | solution.py:858
  144.9 3.9 %collective-permute-done.31.fa = bf16[64,4096]{1,0:T(8,128)(2,1)S(1)} collective-permute-done((bf16[64,4096]{1,0:T(8,128)(2,1)S(1)}, bf16[64,4096]{1,0:T(8,128)(2,1)S(1)}, u32[]{:S(2)}, u32[]{:S(2)}) %collective-permute-start.31) | collective-permute-done | bytes 524320 | tf_op jit(solution)/shard_map/ppermute | solution.py:857
  (58 shorter events, 17.5 us)
Async XLA Ops:
  0.7 10.4 %collective-permute-start.2 = (s32[4]{0:T(128)}, s32[4]{0:T(128)S(1)}, u32[]{:S(2)}, u32[]{:S(2)}) collective-permute-start(s32[4]{0:T(128)} %param.28), channel_id=1, source_target_pairs={{0,0},{4,128},{8,4},{12,132},{16,8},{20,136},{24,12},{28,140},{32,... | collective-permute-start | bytes 56 | tf_op jit(solution)/shard_map/ppermute | solution.py:817
  2.6 8.5 %collective-permute-start.3 = (s32[4]{0:T(128)}, s32[4]{0:T(128)S(1)}, u32[]{:S(2)}, u32[]{:S(2)}) collective-permute-start(s32[4]{0:T(128)} %param.28), channel_id=1, source_target_pairs={{0,128},{4,0},{8,132},{12,4},{16,136},{20,8},{24,140},{28,12},{32,... | collective-permute-start | bytes 56 | tf_op jit(solution)/shard_map/ppermute | solution.py:818
  13.4 8.1 %collective-permute-start.7 = (bf16[1040,128]{1,0:T(8,128)(2,1)S(1)}, bf16[1040,128]{1,0:T(8,128)(2,1)S(1)}, u32[]{:S(2)}, u32[]{:S(2)}) collective-permute-start(bf16[1040,128]{1,0:T(8,128)(2,1)S(1)} %get-tuple-element.1045.refs_4_), channel_id=1, source_target_pairs={{0,16},{4,20},{8,24},{12,28},{16,32},{20,36},{24,40},{28,44},{32,4... | collective-permute-start | bytes 798728 | tf_op jit(solution)/shard_map/ppermute | solution.py:142
  15.2 10.3 %collective-permute-start.11 = (bf16[1040,128]{1,0:T(8,128)(2,1)S(1)}, bf16[1040,128]{1,0:T(8,128)(2,1)S(1)}, u32[]{:S(2)}, u32[]{:S(2)}) collective-permute-start(bf16[1040,128]{1,0:T(8,128)(2,1)S(1)} %get-tuple-element.1045.refs_4_), channel_id=1, source_target_pairs={{0,112},{4,116},{8,120},{12,124},{16,0},{20,4},{24,8},{28,12},{32,... | collective-permute-start | bytes 798728 | tf_op jit(solution)/shard_map/ppermute | solution.py:142
  21.5 9.8 %collective-permute-start.8 = (bf16[1040,128]{1,0:T(8,128)(2,1)S(1)}, bf16[1040,128]{1,0:T(8,128)(2,1)S(1)}, u32[]{:S(2)}, u32[]{:S(2)}) collective-permute-start(bf16[1040,128]{1,0:T(8,128)(2,1)S(1)} %collective-permute-done.7.refs_5_), channel_id=1, source_target_pairs={{0,16},{4,20},{8,24},{12,28},{16,32},{20,36},{24,40},{28,44},{32,4... | collective-permute-start | bytes 798728 | tf_op jit(solution)/shard_map/ppermute | solution.py:142
  25.2 10.4 %collective-permute-start.17 = (bf16[1024,128]{1,0:T(8,128)(2,1)S(1)}, bf16[1024,128]{1,0:T(8,128)(2,1)S(1)}, u32[]{:S(2)}, u32[]{:S(2)}) collective-permute-start(bf16[1024,128]{1,0:T(8,128)(2,1)S(1)} %get-tuple-element.1048.refs_0_), channel_id=1, source_target_pairs={{0,112},{4,116},{8,120},{12,124},{16,0},{20,4},{24,8},{28,12},{32,... | collective-permute-start | bytes 786440 | tf_op jit(solution)/shard_map/ppermute | solution.py:142
  25.5 15.8 %collective-permute-start.12 = (bf16[1040,128]{1,0:T(8,128)(2,1)S(1)}, bf16[1040,128]{1,0:T(8,128)(2,1)S(1)}, u32[]{:S(2)}, u32[]{:S(2)}) collective-permute-start(bf16[1040,128]{1,0:T(8,128)(2,1)S(1)} %collective-permute-done.11.refs_11_), channel_id=1, source_target_pairs={{0,112},{4,116},{8,120},{12,124},{16,0},{20,4},{24,8},{28,12},{32,... | collective-permute-start | bytes 798728 | tf_op jit(solution)/shard_map/ppermute | solution.py:142
  31.3 10.5 %collective-permute-start.9 = (bf16[1040,128]{1,0:T(8,128)(2,1)S(1)}, bf16[1040,128]{1,0:T(8,128)(2,1)S(1)}, u32[]{:S(2)}, u32[]{:S(2)}) collective-permute-start(bf16[1040,128]{1,0:T(8,128)(2,1)S(1)} %collective-permute-done.8.refs_6_), channel_id=1, source_target_pairs={{0,16},{4,20},{8,24},{12,28},{16,32},{20,36},{24,40},{28,44},{32,4... | collective-permute-start | bytes 798728 | tf_op jit(solution)/shard_map/ppermute | solution.py:142
  35.0 12.4 %collective-permute-start.14 = (bf16[1024,128]{1,0:T(8,128)(2,1)S(1)}, bf16[1024,128]{1,0:T(8,128)(2,1)S(1)}, u32[]{:S(2)}, u32[]{:S(2)}) collective-permute-start(bf16[1024,128]{1,0:T(8,128)(2,1)S(1)} %get-tuple-element.1048.refs_0_), channel_id=1, source_target_pairs={{0,16},{4,20},{8,24},{12,28},{16,32},{20,36},{24,40},{28,44},{32,4... | collective-permute-start | bytes 786440 | tf_op jit(solution)/shard_map/ppermute | solution.py:142
  35.6 15.5 %collective-permute-start.18 = (bf16[1024,128]{1,0:T(8,128)(2,1)S(1)}, bf16[1024,128]{1,0:T(8,128)(2,1)S(1)}, u32[]{:S(2)}, u32[]{:S(2)}) collective-permute-start(bf16[1024,128]{1,0:T(8,128)(2,1)S(1)} %collective-permute-done.17.refs_7_), channel_id=1, source_target_pairs={{0,112},{4,116},{8,120},{12,124},{16,0},{20,4},{24,8},{28,12},{32,... | collective-permute-start | bytes 786440 | tf_op jit(solution)/shard_map/ppermute | solution.py:142
  41.3 23.3 %collective-permute-start.13 = (bf16[1040,128]{1,0:T(8,128)(2,1)S(1)}, bf16[1040,128]{1,0:T(8,128)(2,1)S(1)}, u32[]{:S(2)}, u32[]{:S(2)}) collective-permute-start(bf16[1040,128]{1,0:T(8,128)(2,1)S(1)} %collective-permute-done.12.refs_10_), channel_id=1, source_target_pairs={{0,112},{4,116},{8,120},{12,124},{16,0},{20,4},{24,8},{28,12},{32,... | collective-permute-start | bytes 798728 | tf_op jit(solution)/shard_map/ppermute | solution.py:142
  41.8 22.9 %collective-permute-start.10 = (bf16[1040,128]{1,0:T(8,128)(2,1)S(1)}, bf16[1040,128]{1,0:T(8,128)(2,1)S(1)}, u32[]{:S(2)}, u32[]{:S(2)}) collective-permute-start(bf16[1040,128]{1,0:T(8,128)(2,1)S(1)} %collective-permute-done.9.refs_7_), channel_id=1, source_target_pairs={{0,16},{4,20},{8,24},{12,28},{16,32},{20,36},{24,40},{28,44},{32,4... | collective-permute-start | bytes 798728 | tf_op jit(solution)/shard_map/ppermute | solution.py:147
  47.4 22.1 %collective-permute-start.15 = (bf16[1024,128]{1,0:T(8,128)(2,1)S(1)}, bf16[1024,128]{1,0:T(8,128)(2,1)S(1)}, u32[]{:S(2)}, u32[]{:S(2)}) collective-permute-start(bf16[1024,128]{1,0:T(8,128)(2,1)S(1)} %collective-permute-done.14.refs_1_), channel_id=1, source_target_pairs={{0,16},{4,20},{8,24},{12,28},{16,32},{20,36},{24,40},{28,44},{32,4... | collective-permute-start | bytes 786440 | tf_op jit(solution)/shard_map/ppermute | solution.py:142
  51.1 21.6 %collective-permute-start.19 = (bf16[1024,128]{1,0:T(8,128)(2,1)S(1)}, bf16[1024,128]{1,0:T(8,128)(2,1)S(1)}, u32[]{:S(2)}, u32[]{:S(2)}) collective-permute-start(bf16[1024,128]{1,0:T(8,128)(2,1)S(1)} %collective-permute-done.18.refs_6_), channel_id=1, source_target_pairs={{0,112},{4,116},{8,120},{12,124},{16,0},{20,4},{24,8},{28,12},{32,... | collective-permute-start | bytes 786440 | tf_op jit(solution)/shard_map/ppermute | solution.py:142
  51.1 4.9 %collective-permute-start.4 = (s32[8]{0:T(128)S(1)}, s32[8]{0:T(128)S(1)}, u32[]{:S(2)}, u32[]{:S(2)}) collective-permute-start(s32[8]{0:T(128)S(1)} %get-tuple-element.1044.refs_0_.list_ref), channel_id=1, source_target_pairs={{0,12},{4,0},{8,4},{12,8},{16,28},{20,16},{24,20},{28,24},{32,44},... | collective-permute-start | bytes 104 | tf_op jit(solution)/shard_map/ppermute | solution.py:824
  56.0 5.1 %collective-permute-start.5 = (s32[8]{0:T(128)S(1)}, s32[8]{0:T(128)S(1)}, u32[]{:S(2)}, u32[]{:S(2)}) collective-permute-start(s32[8]{0:T(128)S(1)} %get-tuple-element.1044.refs_0_.list_ref), channel_id=1, source_target_pairs={{0,8},{4,12},{8,0},{12,4},{16,24},{20,28},{24,16},{28,20},{32,40},... | collective-permute-start | bytes 104 | tf_op jit(solution)/shard_map/ppermute | solution.py:824
  67.9 16.1 %collective-permute-start.21 = (bf16[1040,128]{1,0:T(8,128)(2,1)S(1)}, bf16[1040,128]{1,0:T(8,128)(2,1)S(1)}, u32[]{:S(2)}, u32[]{:S(2)}) collective-permute-start(bf16[1040,128]{1,0:T(8,128)(2,1)S(1)} %get-tuple-element.1051), channel_id=1, source_target_pairs={{0,4},{4,8},{8,12},{12,0},{16,20},{20,24},{24,28},{28,16},{32,36},... | collective-permute-start | bytes 798728 | tf_op jit(solution)/shard_map/ppermute | solution.py:834
  69.5 7.1 %collective-permute-start.16 = (bf16[1024,128]{1,0:T(8,128)(2,1)S(1)}, bf16[1024,128]{1,0:T(8,128)(2,1)S(1)}, u32[]{:S(2)}, u32[]{:S(2)}) collective-permute-start(bf16[1024,128]{1,0:T(8,128)(2,1)S(1)} %collective-permute-done.15.refs_2_), channel_id=1, source_target_pairs={{0,16},{4,20},{8,24},{12,28},{16,32},{20,36},{24,40},{28,44},{32,4... | collective-permute-start | bytes 786440 | tf_op jit(solution)/shard_map/ppermute | solution.py:142
  72.7 7.6 %collective-permute-start.20 = (bf16[1024,128]{1,0:T(8,128)(2,1)S(1)}, bf16[1024,128]{1,0:T(8,128)(2,1)S(1)}, u32[]{:S(2)}, u32[]{:S(2)}) collective-permute-start(bf16[1024,128]{1,0:T(8,128)(2,1)S(1)} %collective-permute-done.19.refs_5_), channel_id=1, source_target_pairs={{0,112},{4,116},{8,120},{12,124},{16,0},{20,4},{24,8},{28,12},{32,... | collective-permute-start | bytes 786440 | tf_op jit(solution)/shard_map/ppermute | solution.py:148
  72.7 20.6 %collective-permute-start.22 = (bf16[1040,128]{1,0:T(8,128)(2,1)S(1)}, bf16[1040,128]{1,0:T(8,128)(2,1)S(1)}, u32[]{:S(2)}, u32[]{:S(2)}) collective-permute-start(bf16[1040,128]{1,0:T(8,128)(2,1)S(1)} %get-tuple-element.1052), channel_id=1, source_target_pairs={{0,8},{4,12},{8,0},{12,4},{16,24},{20,28},{24,16},{28,20},{32,40},... | collective-permute-start | bytes 798728 | tf_op jit(solution)/shard_map/ppermute | solution.py:834
  73.6 19.6 %collective-permute-start.23 = (bf16[1040,128]{1,0:T(8,128)(2,1)S(1)}, bf16[1040,128]{1,0:T(8,128)(2,1)S(1)}, u32[]{:S(2)}, u32[]{:S(2)}) collective-permute-start(bf16[1040,128]{1,0:T(8,128)(2,1)S(1)} %get-tuple-element.1053), channel_id=1, source_target_pairs={{0,12},{4,0},{8,4},{12,8},{16,28},{20,16},{24,20},{28,24},{32,44},... | collective-permute-start | bytes 798728 | tf_op jit(solution)/shard_map/ppermute | solution.py:834
  81.3 20.2 %collective-permute-start.24 = (bf16[1024,128]{1,0:T(8,128)(2,1)S(1)}, bf16[1024,128]{1,0:T(8,128)(2,1)S(1)}, u32[]{:S(2)}, u32[]{:S(2)}) collective-permute-start(bf16[1024,128]{1,0:T(8,128)(2,1)S(1)} %get-tuple-element.1056), channel_id=1, source_target_pairs={{0,4},{4,8},{8,12},{12,0},{16,20},{20,24},{24,28},{28,16},{32,36},... | collective-permute-start | bytes 786440 | tf_op jit(solution)/shard_map/ppermute | solution.py:838
  81.4 20.0 %collective-permute-start.25 = (bf16[1024,128]{1,0:T(8,128)(2,1)S(1)}, bf16[1024,128]{1,0:T(8,128)(2,1)S(1)}, u32[]{:S(2)}, u32[]{:S(2)}) collective-permute-start(bf16[1024,128]{1,0:T(8,128)(2,1)S(1)} %get-tuple-element.1057), channel_id=1, source_target_pairs={{0,8},{4,12},{8,0},{12,4},{16,24},{20,28},{24,16},{28,20},{32,40},... | collective-permute-start | bytes 786440 | tf_op jit(solution)/shard_map/ppermute | solution.py:838
  84.0 17.5 %collective-permute-start.26 = (bf16[1024,128]{1,0:T(8,128)(2,1)S(1)}, bf16[1024,128]{1,0:T(8,128)(2,1)S(1)}, u32[]{:S(2)}, u32[]{:S(2)}) collective-permute-start(bf16[1024,128]{1,0:T(8,128)(2,1)S(1)} %get-tuple-element.1058), channel_id=1, source_target_pairs={{0,12},{4,0},{8,4},{12,8},{16,28},{20,16},{24,20},{28,24},{32,44},... | collective-permute-start | bytes 786440 | tf_op jit(solution)/shard_map/ppermute | solution.py:838
  115.6 9.8 %collective-permute-start.33 = (bf16[64,2048]{1,0:T(8,128)(2,1)S(1)}, bf16[64,2048]{1,0:T(8,128)(2,1)S(1)}, u32[]{:S(2)}, u32[]{:S(2)}) collective-permute-start(bf16[64,2048]{1,0:T(8,128)(2,1)S(1)} %get-tuple-element.1076), channel_id=1, source_target_pairs={{0,3},{1,0},{2,1},{3,2},{4,7},{5,4},{6,5},{7,6},{8,11},{9,8},{10,9... | collective-permute-start | bytes 786440 | tf_op jit(solution)/shard_map/ppermute | solution.py:854
  118.7 12.3 %collective-permute-start.32 = (bf16[64,2048]{1,0:T(8,128)(2,1)S(1)}, bf16[64,2048]{1,0:T(8,128)(2,1)S(1)}, u32[]{:S(2)}, u32[]{:S(2)}) collective-permute-start(bf16[64,2048]{1,0:T(8,128)(2,1)S(1)} %get-tuple-element.1075), channel_id=1, source_target_pairs={{0,3},{1,0},{2,1},{3,2},{4,7},{5,4},{6,5},{7,6},{8,11},{9,8},{10,9... | collective-permute-start | bytes 786440 | tf_op jit(solution)/shard_map/ppermute | solution.py:851
  119.5 15.5 %collective-permute-start.30 = (bf16[64,2048]{1,0:T(8,128)(2,1)S(1)}, bf16[64,2048]{1,0:T(8,128)(2,1)S(1)}, u32[]{:S(2)}, u32[]{:S(2)}) collective-permute-start(bf16[64,2048]{1,0:T(8,128)(2,1)S(1)} %get-tuple-element.1073), channel_id=1, source_target_pairs={{0,1},{1,2},{2,3},{3,0},{4,5},{5,6},{6,7},{7,4},{8,9},{9,10},{10,1... | collective-permute-start | bytes 786440 | tf_op jit(solution)/shard_map/ppermute | solution.py:853
  120.8 14.7 %collective-permute-start.29 = (bf16[64,2048]{1,0:T(8,128)(2,1)S(1)}, bf16[64,2048]{1,0:T(8,128)(2,1)S(1)}, u32[]{:S(2)}, u32[]{:S(2)}) collective-permute-start(bf16[64,2048]{1,0:T(8,128)(2,1)S(1)} %get-tuple-element.1072), channel_id=1, source_target_pairs={{0,1},{1,2},{2,3},{3,0},{4,5},{5,6},{6,7},{7,4},{8,9},{9,10},{10,1... | collective-permute-start | bytes 786440 | tf_op jit(solution)/shard_map/ppermute | solution.py:850
  120.8 18.5 %collective-permute-start.27 = (bf16[64,4096]{1,0:T(8,128)(2,1)S(1)}, bf16[64,4096]{1,0:T(8,128)(2,1)S(1)}, u32[]{:S(2)}, u32[]{:S(2)}) collective-permute-start(bf16[64,4096]{1,0:T(8,128)(2,1)S(1)} %get-tuple-element.1069), channel_id=1, source_target_pairs={{0,3},{1,0},{2,1},{3,2},{4,7},{5,4},{6,5},{7,6},{8,11},{9,8},{10,9... | collective-permute-start | bytes 1572872 | tf_op jit(solution)/shard_map/ppermute | solution.py:855
  125.4 17.7 %collective-permute-start.28 = (bf16[64,4096]{1,0:T(8,128)(2,1)S(1)}, bf16[64,4096]{1,0:T(8,128)(2,1)S(1)}, u32[]{:S(2)}, u32[]{:S(2)}) collective-permute-start(bf16[64,4096]{1,0:T(8,128)(2,1)S(1)} %get-tuple-element.1070), channel_id=1, source_target_pairs={{0,1},{1,2},{2,3},{3,0},{4,5},{5,6},{6,7},{7,4},{8,9},{9,10},{10,1... | collective-permute-start | bytes 1572872 | tf_op jit(solution)/shard_map/ppermute | solution.py:856
  131.2 13.7 %collective-permute-start.34 = (bf16[64,4096]{1,0:T(8,128)(2,1)S(1)}, bf16[64,4096]{1,0:T(8,128)(2,1)S(1)}, u32[]{:S(2)}, u32[]{:S(2)}) collective-permute-start(bf16[64,4096]{1,0:T(8,128)(2,1)S(1)} %combine.3), channel_id=1, source_target_pairs={{0,3},{1,0},{2,1},{3,2},{4,7},{5,4},{6,5},{7,6},{8,11},{9,8},{10,9... | collective-permute-start | bytes 1572872 | tf_op jit(solution)/shard_map/ppermute | solution.py:858
  135.6 13.2 %collective-permute-start.31 = (bf16[64,4096]{1,0:T(8,128)(2,1)S(1)}, bf16[64,4096]{1,0:T(8,128)(2,1)S(1)}, u32[]{:S(2)}, u32[]{:S(2)}) collective-permute-start(bf16[64,4096]{1,0:T(8,128)(2,1)S(1)} %combine.2), channel_id=1, source_target_pairs={{0,1},{1,2},{2,3},{3,0},{4,5},{5,6},{6,7},{7,4},{8,9},{9,10},{10,1... | collective-permute-start | bytes 1572872 | tf_op jit(solution)/shard_map/ppermute | solution.py:857
  (6 other events, 168.0 us)
